TPU v7x, 256 devices: a whole 4x4x8 slice. The times are simulated.
256 devices in a mesh: row: 16 (over y, z_lo, core), col: 16 (over z_hi, x).
Axes of the slice: x: 4, y: 4, z: 8 (z_hi: 4, z_lo: 2; z = z_hi * 2 + z_lo), core: 2. Of those that a mesh axis runs over, the one named last changes fastest.
Arguments:
- tokens: bfloat16 [4096, 8192], P('col', 'row'), may hold values from -6 to 6
- grad_out: bfloat16 [4096, 16384], P('row', 'col'), may hold values from -6 to 6
- base_weight: float32 [8192, 16384], P('row', 'col'), may hold values from -6 to 6
- left_param: float32 [16, 512, 512], P('row'), may hold values from -6 to 6
- right_param: float32 [64, 256, 256], P('col'), may hold values from -6 to 6
Outputs:
- rotated_weight: float32 [8192, 16384], P('row', 'col')
- new_left: float32 [16, 512, 512], P('row')
- new_right: float32 [64, 256, 256], P('col')
All inputs are finite; a program needn't handle non-finite values.
Results may differ from a plain program's by a relative error of at most 0.0003.
Values may be sent and summed in bfloat16 or wider, within the bound.
A program may use at most 128 MiB of HBM per device.

v0:
```python
import math

import jax
import jax.numpy as jnp
from jax import lax
from jax.sharding import PartitionSpec as P

precise = lax.Precision.HIGHEST
taylor_degree = 6
step_rate = 0.3
epsilon = 1e-06


def batch_product(first, second):
    return jnp.einsum("lab,lbc->lac", first, second, precision=precise)


def transpose_last(matrix):
    return jnp.swapaxes(matrix, 1, 2)


def skew_from(param):
    skew_scale = 0.5 / math.sqrt(param.shape[-1])
    return skew_scale * (param - transpose_last(param))


def column_levels(skew, col_start, col_width):
    dimension = skew.shape[-1]
    eye_part = (
        jnp.arange(dimension)[:, None] == col_start + jnp.arange(col_width)[None, :]
    ).astype(jnp.float32)
    current = (
        eye_part[None] + lax.dynamic_slice_in_dim(skew, col_start, col_width, 2) / taylor_degree
    )
    horner_levels = [current] * (taylor_degree + 1)
    for divisor in range(taylor_degree - 1, 0, -1):
        current = eye_part[None] + batch_product(skew, current) / divisor
        horner_levels[divisor] = current
    return horner_levels


def adjoint(skew, horner_levels, upper_grad):
    running = jnp.zeros(skew.shape, jnp.float32)
    for divisor in range(1, taylor_degree):
        running = (
            running
            + batch_product(upper_grad, transpose_last(horner_levels[divisor + 1])) / divisor
        )
        upper_grad = batch_product(transpose_last(skew), upper_grad) / divisor
    return (running, upper_grad)


def update_param(param, accum):
    skew_scale = 0.5 / math.sqrt(param.shape[-1])
    grad_param = skew_scale * (accum - transpose_last(accum))
    root_mean = jnp.sqrt(jnp.mean(grad_param * grad_param, axis=(1, 2), keepdims=True) + epsilon)
    return param - step_rate * grad_param / root_mean


def right_apply(weight, rotation):
    count = rotation.shape[0]
    block = rotation.shape[-1]
    shaped = weight.reshape(weight.shape[0], count, block)
    return jnp.einsum("nbr,brs->nbs", shaped, rotation, precision=precise).reshape(weight.shape)


def body(tokens, grad_out, base_weight, left_param, right_param):
    col_count = lax.axis_size("col")
    left_size = left_param.shape[-1]
    left_count = left_param.shape[0]
    right_size = right_param.shape[-1]
    right_count = right_param.shape[0]
    row_total = base_weight.shape[0]
    col_total = base_weight.shape[1]
    col_width = left_size // col_count
    col_start = lax.axis_index("col") * col_width
    left_skew = skew_from(left_param)
    right_skew = skew_from(right_param)
    left_cols = column_levels(left_skew, col_start, col_width)
    right_levels = column_levels(right_skew, 0, right_size)
    right_rot = right_levels[1]
    token_all = lax.all_gather(tokens, "col", axis=0, tiled=True)
    left_rot = lax.all_gather(left_cols[1], "col", axis=2, tiled=True)
    grads_all = lax.all_gather(grad_out, "row", axis=0, tiled=True)
    grad_weight = lax.dot_general(
        token_all, grads_all, (((0,), (0,)), ((), ())), preferred_element_type=jnp.float32
    )
    weight_blocks = base_weight.reshape(left_count, left_size, col_total)
    grad_blocks = grad_weight.reshape(left_count, left_size, col_total)
    mixed_weight = right_apply(base_weight, right_rot).reshape(left_count, left_size, col_total)
    left_part = jnp.einsum("lnc,lmc->lnm", grad_blocks, mixed_weight, precision=precise)
    rotated = batch_product(left_rot, weight_blocks).reshape(row_total, right_count, right_size)
    right_part = jnp.einsum(
        "nbr,nbs->brs",
        rotated,
        grad_weight.reshape(row_total, right_count, right_size),
        precision=precise,
    )
    right_grad = lax.psum(right_part, "row")
    upper_piece = lax.psum_scatter(left_part, "col", scatter_dimension=2, tiled=True)
    partial_sum, upper_piece = adjoint(left_skew, left_cols, upper_piece)
    placed = lax.dynamic_update_slice_in_dim(
        jnp.zeros_like(partial_sum), upper_piece / taylor_degree, col_start, 2
    )
    left_acc = lax.psum(partial_sum + placed, "col")
    right_acc, right_upper = adjoint(right_skew, right_levels, right_grad)
    right_acc = right_acc + right_upper / taylor_degree
    new_left = update_param(left_param, left_acc)
    new_right = update_param(right_param, right_acc)
    new_left_skew = skew_from(new_left)
    new_cols = column_levels(new_left_skew, col_start, col_width)[1]
    new_left_rot = lax.all_gather(new_cols, "col", axis=2, tiled=True)
    new_right_rot = column_levels(skew_from(new_right), 0, right_size)[1]
    turned = batch_product(new_left_rot, weight_blocks).reshape(row_total, col_total)
    rotated_weight = right_apply(turned, new_right_rot)
    return (rotated_weight, new_left, new_right)


def solution(mesh):
    return jax.shard_map(
        body,
        mesh=mesh,
        in_specs=(
            P("col", "row"),
            P("row", "col"),
            P("row", "col"),
            P("row", None, None),
            P("col", None, None),
        ),
        out_specs=(P("row", "col"), P("row", None, None), P("col", None, None)),
        check_vma=False,
    )
```

profile of v0, /device:TPU:32, one launch (start us, length us, event | category | flops | bytes accessed | tf_op | source)
XLA Modules:
  0.0 774.6 jit_solution(18041137845352495483)
XLA Ops:
  8.7 1.6 copy.29
  13.6 1.3 convolution_add_fusion.3
  16.0 1.3 copy.31
  17.3 1.7 bitcast_subtract_fusion.4
  19.1 1.9 fusion.28
  21.0 1.9 fusion.27
  23.0 1.9 fusion.26
  25.9 1.9 fusion.25
  28.8 1.9 convolution_add_fusion
  30.8 5.1 fusion
  35.8 53.9 %all-gather.7.cloned.1.call-done = bf16[4096,512]{1,0:T(8,128)(2,1)} async-done(((bf16[256,512]{1,0:T(8,128)(2,1)}), bf16[4096,512]{1,0:T(8,128)(2,1)}) %all-gather.7.cloned.1.call-update) | async-done | bytes 4194320 | tf_op jit(solution)/shard_map/all_gather | solution.py:82
  89.7 55.2 %all-gather.9.cloned.1.call-done = bf16[4096,1024]{1,0:T(8,128)(2,1)} async-done(((bf16[256,1024]{1,0:T(8,128)(2,1)}), bf16[4096,1024]{1,0:T(8,128)(2,1)}) %all-gather.9.cloned.1.call-update) | async-done | bytes 8388624 | tf_op jit(solution)/shard_map/all_gather | solution.py:84
  144.9 8.3 %fusion.122 = f32[512,1024]{1,0:T(8,128)S(1)} fusion(bf16[4096,512]{1,0:T(8,128)(2,1)} %all-gather.7.cloned.1.call-done, bf16[4096,1024]{1,0:T(8,128)(2,1)} %all-gather.9.cloned.1.call-done), kind=kOutput, calls=%fused_computation.176 | convolution fusion | flops 4294967296 | bytes 14680064 | tf_op jit(solution)/shard_map/dot_general | solution.py:85
  153.3 1.3 copy-done.17
  154.6 4.5 convolution_bitcast_fusion
  159.1 3.6 copy.45
  162.7 37.1 %all-gather.11.cloned.1.call-done = f32[512,512]{0,1:T(8,128)} async-done(((f32[512,32]{0,1:T(8,128)}), f32[512,512]{0,1:T(8,128)}) %all-gather.11.cloned.1.call-update) | async-done | bytes 1048592 | tf_op jit(solution)/shard_map/all_gather | solution.py:83
  199.8 5.5 fusion.7
  205.4 3.1 fusion.2
  210.3 160.0 %all-reduce.9.cloned.1.call-done = f32[1,512,512]{1,0,2:T(1,128)} async-done(((f32[1,512,512]{1,0,2:T(1,128)}), f32[1,512,512]{1,0,2:T(1,128)}) %all-reduce.9.cloned.1.call-update) | async-done | bytes 1048592
  371.1 1.7 fusion.52
  372.8 2.8 fusion.84
  375.6 119.3 %all-reduce.5.cloned.1.call-done = f32[4,256,256]{2,1,0:T(8,128)} async-done(((f32[4,256,256]{2,1,0:T(8,128)}), f32[4,256,256]{2,1,0:T(8,128)}) %all-reduce.5.cloned.1.call-update) | async-done | bytes 1048592 | tf_op jit(solution)/shard_map/psum | solution.py:99
  494.9 2.4 fusion.78
  499.7 2.1 convolution_multiply_fusion.10
  504.3 1.2 fusion.23
  505.6 2.2 fusion.22
  508.8 1.2 convolution_multiply_fusion.26
  516.5 1.7 fusion.35
  518.3 3.0 fusion.21
  521.2 2.2 fusion.20
  523.4 1.6 copy.39
  526.2 1.6 copy.40
  527.8 162.6 %all-reduce.7.cloned.1.call-done = f32[1,512,512]{1,2,0:T(8,128)} async-done(((f32[1,512,512]{1,2,0:T(8,128)}), f32[1,512,512]{1,2,0:T(8,128)}) %all-reduce.7.cloned.1.call-update) | async-done | bytes 1048592 | tf_op jit(solution)/shard_map/psum | solution.py:105
  690.3 2.6 copy.46
  693.0 3.0 multiply_reduce_fusion
  696.7 2.5 copy.47
  699.2 1.5 divide_subtract_fusion
  704.6 1.3 convolution_add_fusion.2
  707.5 1.9 fusion.19
  709.5 2.1 fusion.18
  711.6 1.9 fusion.17
  713.6 1.9 fusion.16
  715.5 2.9 convolution_add_fusion.1
  718.4 39.1 %all-gather.13.cloned.1.call-done = f32[512,512]{0,1:T(8,128)} async-done(((f32[512,32]{0,1:T(8,128)}), f32[512,512]{0,1:T(8,128)}) %all-gather.13.cloned.1.call-update) | async-done | bytes 1048592 | tf_op jit(solution)/shard_map/all_gather | solution.py:112
  757.5 4.7 fusion.5
  762.2 3.5 fusion.124
  765.7 1.8 copy.50
  (107 shorter events, 28.6 us)
Async XLA Ops:
  7.2 3.1 copy-start.2
  7.2 82.5 %all-gather.7.cloned.1.call-start = ((), (), s32[]{:S(2)}) async-start(), calls=%async_computation | async-start | bytes 4456448 | tf_op jit(solution)/shard_map/all_gather | solution.py:82
  7.9 137.0 %all-gather.9.cloned.1.call-start = ((), (), s32[]{:S(2)}) async-start(), calls=%async_computation.1 | async-start | bytes 8912896 | tf_op jit(solution)/shard_map/all_gather | solution.py:84
  8.7 191.2 %all-gather.11.cloned.1.call-start = ((), (), s32[]{:S(2)}) async-start(), calls=%async_computation.4 | async-start | bytes 1114112 | tf_op jit(solution)/shard_map/all_gather | solution.py:83
  12.0 4.0 copy-start.3
  12.8 2.1 copy-start.26
  13.5 1.4 copy-start.28
  14.9 355.3 %all-reduce.9.cloned.1.call-start = ((), (), s32[]{:S(2)}) async-start(), calls=%async_computation.6 | async-start | bytes 2097152
  17.3 1.7 copy-start.20
  21.0 1.9 copy-start.10
  23.0 1.9 copy-start.12
  24.9 1.0 copy-start.14
  27.8 1.0 copy-start.5
  28.8 1.9 copy-start
  144.9 9.7 %copy-start.19 = (f32[4,256,512]{2,1,0:T(8,128)S(1)}, f32[4,256,512]{2,1,0:T(8,128)}, u32[]{:S(2)}) copy-start(f32[4,256,512]{2,1,0:T(8,128)} %fusion) | copy-start | bytes 6291460
  153.3 1.3 copy-start.17
  162.7 332.2 %all-reduce.5.cloned.1.call-start = ((), (), s32[]{:S(2)}) async-start(), calls=%async_computation.2 | async-start | bytes 2097152 | tf_op jit(solution)/shard_map/psum | solution.py:99
  199.8 5.6 copy-start.18
  205.4 3.6 copy-start.30
  208.5 481.8 %all-reduce.7.cloned.1.call-start = ((), (), s32[]{:S(2)}) async-start(), calls=%async_computation.3 | async-start | bytes 2097152 | tf_op jit(solution)/shard_map/psum | solution.py:105
  499.7 2.2 copy-start.6
  499.7 2.2 copy-start.22
  501.9 1.2 copy-start.15
  503.1 1.2 copy-start.13
  504.3 1.2 copy-start.11
  505.6 2.2 copy-start.29
  507.7 3.4 copy-start.24
  507.7 3.4 copy-start.27
  518.2 3.0 copy-start.8
  518.2 239.3 %all-gather.13.cloned.1.call-start = ((), (), s32[]{:S(2)}) async-start(), calls=%async_computation.5 | async-start | bytes 1114112 | tf_op jit(solution)/shard_map/all_gather | solution.py:112
  523.4 1.7 copy-start.16
  690.3 2.6 copy-start.25
  700.7 1.0 copy-start.7
  703.1 2.9 copy-start.4
  706.2 1.0 copy-start.9
  706.6 1.0 copy-start.21
  715.5 42.0 %copy-start.1 = (f32[512,1024]{1,0:T(8,128)S(1)}, f32[512,1024]{1,0:T(8,128)}, u32[]{:S(2)}) copy-start(f32[512,1024]{1,0:T(8,128)} %param.7) | copy-start | bytes 6291460
  718.4 43.8 %copy-start.23 = (f32[4,256,256]{2,1,0:T(8,128)S(1)}, f32[4,256,256]{2,1,0:T(8,128)}, u32[]{:S(2)}) copy-start(f32[4,256,256]{2,1,0:T(8,128)} %convolution_add_fusion.1) | copy-start | bytes 3145732
Sparse Core Ops, SparseCore 0:
  10.4 79.2 all-gather.6
  91.6 53.3 all-gather.8
  147.4 52.4 all-gather.10
  202.3 167.8 all-reduce.8
  373.3 121.5 all-reduce.4
  518.3 171.9 all-reduce.6
  706.1 51.3 all-gather.12
where the time goes:
time: 781 us; the launch traced here: 775 us
  waiting for transfers between devices  629 us (81%)
  matrix products  95.5 us (12%)
  local copies, waits for them, and re-layouts  25.2 us (3%)
  between operations  16.4 us (2%)
  other arithmetic  8.11 us (1%)
    psum x1, waiting for transfers between devices, body(): left_acc = lax.psum(partial_sum + placed, 'col')  163 us
    unnamed x8, waiting for transfers between devices  161 us
    psum x1, waiting for transfers between devices, body(): right_grad = lax.psum(right_part, 'row')  119 us
    dot_general x42, matrix products, batch_product(): return jnp.einsum('lab,lbc->lac', first, second, precision=precise)  71 us
    all_gather x1, waiting for transfers between devices, body(): grads_all = lax.all_gather(grad_out, 'row', axis=0, tiled=True)  55.2 us
    all_gather x1, waiting for transfers between devices, body(): token_all = lax.all_gather(tokens, 'col', axis=0, tiled=True)  53.9 us
    all_gather x1, waiting for transfers between devices, body(): new_left_rot = lax.all_gather(new_cols, 'col', axis=2, tiled=True)  39.1 us
    all_gather x1, waiting for transfers between devices, body(): left_rot = lax.all_gather(left_cols[1], 'col', axis=2, tiled=True)  37.1 us
  transfers between devices with their start and end apart: 7, of which 7 were waited for; matrix products, arithmetic and copies ran while one was open for 10% of the time, Pallas kernels for 0%

commit v1 on v0

v1 whole, which is shorter than its diff:
```python
import math

import jax
import jax.numpy as jnp
from jax import lax
from jax.experimental import pallas as pl
from jax.experimental.pallas import tpu as pltpu
from jax.sharding import PartitionSpec as P

step_rate = 0.3
epsilon = 1e-06
f32 = jnp.float32
bf16 = jnp.bfloat16
C2, C3, C4, C5, C6 = 1 / 2, 1 / 6, 1 / 24, 1 / 120, 1 / 720
LB, RB = 512, 256
NN = (((1,), (0,)), ((), ()))
NT = (((1,), (1,)), ((), ()))


def split(value):
    high = value.astype(bf16)
    return high, (value - high.astype(f32)).astype(bf16)


def put(pair, value, where=Ellipsis):
    pair[0][where], pair[1][where] = split(value)


def dot(first, second, dims=NN):
    return lax.dot_general(first, second, dims, preferred_element_type=f32)


def dot3(first, second, dims=NN):
    ah, al = first
    bh, bl = second
    return dot(ah, bh, dims) + (dot(ah, bl, dims) + dot(al, bh, dims))


def get(pair, where=Ellipsis):
    return pair[0][where], pair[1][where]


def rows_loop(total, tile, fn):
    def step(index, carry):
        fn(pl.ds(pl.multiple_of(index * tile, tile), tile))
        return carry

    lax.fori_loop(0, total // tile, step, 0)


def eye(rows, size):
    r = lax.broadcasted_iota(jnp.int32, (rows.size, size), 0) + rows.start
    c = lax.broadcasted_iota(jnp.int32, (rows.size, size), 1)
    return jnp.where(r == c, 1.0, 0.0).astype(f32)


def poly(size, tile, S, SP, AP, BP, CP, Af, finish, CT=None):
    def square(rows):
        a = dot3(get(SP, rows), get(SP))
        Af[rows] = a
        put(AP, a, rows)

    rows_loop(size, tile, square)

    def cube(rows):
        b = dot3(get(SP, rows), get(AP))
        put(BP, b, rows)
        s = S[rows]
        a = Af[rows]
        even = C3 * eye(rows, size) + C5 * a
        odd = C4 * s + C6 * b
        put(CP, even + odd, rows)
        if CT is not None:
            put(CT, even - odd, rows)

    rows_loop(size, tile, cube)

    def last(rows):
        finish(rows, eye(rows, size) + S[rows] + C2 * Af[rows] + dot3(get(BP, rows), get(CP)))

    rows_loop(size, tile, last)


def adjoint(size, tile, G, GP, SP, AP, BP, CT, EP, Ea, Aa, Eb):
    put(GP, G[...])

    def first(rows):
        c_bar = -dot3(get(BP, rows), get(GP))
        b_bar = dot3(get(GP, rows), get(CT)) + C6 * c_bar
        put(EP, b_bar, rows)
        g = G[rows]
        Ea[rows] = g + C4 * c_bar
        Aa[rows] = C2 * g + C5 * c_bar

    rows_loop(size, tile, first)

    def second(rows):
        Ea[rows] += dot3(get(EP, rows), get(AP))
        Aa[rows] -= dot3(get(SP, rows), get(EP))

    rows_loop(size, tile, second)
    a_bar = Aa[...]
    put(GP, a_bar + a_bar.T)

    def third(rows):
        Eb[rows] = Ea[rows] - dot3(get(GP, rows), get(SP))

    rows_loop(size, tile, third)
    e = Eb[...]
    return e - e.T


def updated(param, diff, size):
    p = (0.5 / math.sqrt(size)) * diff
    mean = jnp.sum(p * p) * (1.0 / (size * size))
    return param - step_rate * p / jnp.sqrt(mean + epsilon)


def comm_kernel(
    tok_ref, grad_ref, w_ref, lp_ref, rp_ref, nl_ref, nr_ref,
    T, Gr, gw, gwh, gwl, mh, ml, qh, ql, lw,
    lS, lA, lsh, lsl, lah, lal, lbh, lbl, lch, lcl, lth, ltl, lrh, lrl, lgh, lgl,
    rS, rA, rsh, rsl, rah, ral, rbh, rbl, rch, rcl, rth, rtl, rrh, rrl,
    lpart, xr, xs, Q, zr, zs, Fx,
    rpart, rc, rq, yr, ys, ro, rz, Fy,
    t_recv, t_send, g_recv, g_send, loc_sem,
    xr_sem, zr_sem, za_sem, xa_sem, l_send,
    rc_sem, yr_sem, rz_sem, ya_sem, ra_sem, r_send,
):
    row = lax.axis_index("row")
    col = lax.axis_index("col")
    y, z, c = row // 4, (row // 2) % 2, row % 2
    h, x = col // 4, col % 4

    def row_of(yy, zz, cc):
        return (lax.rem(yy + 4, 4) * 2 + zz) * 2 + cc

    def col_of(hh, xx):
        return lax.rem(hh + 4, 4) * 4 + lax.rem(xx + 4, 4)

    YP, YM = {"row": row_of(y + 1, z, c)}, {"row": row_of(y + 3, z, c)}
    ZZ, CC = {"row": row_of(y, 1 - z, c)}, {"row": row_of(y, z, 1 - c)}
    XP, XM = {"col": col_of(h, x + 1)}, {"col": col_of(h, x + 3)}
    HP, HM = {"col": col_of(h + 1, x)}, {"col": col_of(h + 3, x)}
    started = []

    def send(src, dst, sems, recv, dev):
        counter = sems[1]
        copy = pltpu.make_async_remote_copy(
            src_ref=src, dst_ref=dst, send_sem=sems[0].at[counter[0]], recv_sem=recv,
            device_id=dev, device_id_type=pl.DeviceIdType.MESH,
        )
        counter[0] += 1
        copy.start()
        started.append(copy)

    def arrive(dst, recv):
        pltpu.make_async_remote_copy(
            src_ref=dst, dst_ref=dst, send_sem=loc_sem.at[2], recv_sem=recv,
            device_id=CC, device_id_type=pl.DeviceIdType.MESH,
        ).wait_recv()

    ts, gs, ls, rs = (t_send, [0]), (g_send, [0]), (l_send, [0]), (r_send, [0])

    barrier = pltpu.get_barrier_semaphore()
    for dev in (YP, YM, ZZ, CC, XP, XM, HP, HM):
        pl.semaphore_signal(barrier, inc=1, device_id=dev, device_id_type=pl.DeviceIdType.MESH)
    pl.semaphore_wait(barrier, 8)

    def t_half(ref, half):
        return ref.at[pl.ds(256 * half, 256)]

    def g_half(ref, half):
        return ref.at[pl.ds(128 * half, 128)]

    def t_go(shard, half, dev, own=False):
        src = t_half(tok_ref if own else T.at[shard], half)
        send(src, t_half(T.at[shard], half), ts, t_recv.at[shard, half], dev)

    def t_in(shard, half):
        arrive(t_half(T.at[shard], half), t_recv.at[shard, half])

    def g_go(shard, half, dev, own=False):
        src = g_half(grad_ref if own else Gr.at[shard], half)
        send(src, g_half(Gr.at[shard], half), gs, g_recv.at[shard, half], dev)

    def g_in(shard, half):
        arrive(g_half(Gr.at[shard], half), g_recv.at[shard, half])

    for half in (0, 1):
        t_go(col, half, XP, True)
        t_go(col, 1 - half, XM, True)
        t_go(col, half, HP, True)
        t_go(col, 1 - half, HM, True)
        g_go(row, half, YP, True)
        g_go(row, 1 - half, YM, True)
    for half in (0, 1):
        g_go(row, half, ZZ, True)
        g_go(row, half, CC, True)
    local_t = pltpu.make_async_copy(tok_ref, T.at[col], loc_sem.at[0])
    local_g = pltpu.make_async_copy(grad_ref, Gr.at[row], loc_sem.at[1])
    local_t.start()
    local_g.start()

    def t_ring(hh):
        a, b = col_of(hh, x + 3), col_of(hh, x + 1)
        t_in(a, 0)
        t_go(a, 0, XP)
        t_in(b, 1)
        t_go(b, 1, XM)

    def t_rest(hh):
        t_in(col_of(hh, x + 3), 1)
        t_in(col_of(hh, x + 1), 0)
        t_in(col_of(hh, x + 2), 0)
        t_in(col_of(hh, x + 2), 1)

    def t_spread(shard):
        t_go(shard, 0, XP)
        t_go(shard, 1, XM)
        t_go(shard, 1, XP)
        t_go(shard, 0, XM)

    def g_ring(zz):
        a, b = row_of(y + 3, zz, c), row_of(y + 1, zz, c)
        g_in(a, 0)
        g_go(a, 0, YP)
        g_go(a, 0, CC)
        g_in(b, 1)
        g_go(b, 1, YM)
        g_go(b, 1, CC)

    def g_rest(zz):
        a, b = row_of(y + 3, zz, c), row_of(y + 1, zz, c)
        g_in(a, 1)
        g_go(a, 1, CC)
        g_in(b, 0)
        g_go(b, 0, CC)

    def g_far(zz):
        far = row_of(y + 2, zz, c)
        for half in (0, 1):
            g_in(far, half)
            g_go(far, half, CC)

    lSP, lAP, lBP, lCP, lCT = (lsh, lsl), (lah, lal), (lbh, lbl), (lch, lcl), (lth, ltl)
    lRP, lGP = (lrh, lrl), (lgh, lgl)
    MP, QP, GWP = (mh, ml), (qh, ql), (gwh, gwl)

    def at(pair, index):
        return tuple(ref.at[index] for ref in pair)

    rSP, rAP, rBP, rCP, rCT = (rsh, rsl), (rah, ral), (rbh, rbl), (rch, rcl), (rth, rtl)
    rRP = (rrh, rrl)


    def right_one(index, carry):
        param = rp_ref[index]
        s = (0.5 / math.sqrt(RB)) * (param - param.T)
        rS[index] = s
        put(at(rSP, index), s)
        poly(
            RB, RB, rS.at[index], at(rSP, index), at(rAP, index), at(rBP, index), at(rCP, index), rA.at[index],
            lambda rows, value: put(at(rRP, index), value, rows), at(rCT, index),
        )
        return carry

    lax.fori_loop(0, 1, right_one, 0)
    t_ring(h)
    lax.fori_loop(1, 2, right_one, 0)
    g_ring(z)
    lax.fori_loop(2, 4, right_one, 0)

    t_in(col_of(h + 3, x), 0)
    t_go(col_of(h + 3, x), 0, HP)
    t_in(col_of(h + 1, x), 1)
    t_go(col_of(h + 1, x), 1, HM)
    t_in(col_of(h + 3, x), 1)
    t_spread(col_of(h + 3, x))
    t_in(col_of(h + 1, x), 0)
    t_spread(col_of(h + 1, x))

    param = lp_ref[...]
    s = (0.5 / math.sqrt(LB)) * (param - param.T)
    lS[...] = s
    put(lSP, s)

    other = row_of(y, 1 - z, c)
    for half in (0, 1):
        g_in(other, half)
    g_go(other, 0, YP)
    g_go(other, 1, YM)
    g_go(other, 1, YP)
    g_go(other, 0, YM)
    g_go(other, 0, CC)
    g_go(other, 1, CC)
    g_rest(z)

    def weight_right(rows):
        for index in range(4):
            cols = slice(RB * index, RB * (index + 1))
            m = dot3(split(w_ref[rows, cols]), get(at(rRP, index)))
            mh[rows, cols], ml[rows, cols] = split(m)

    rows_loop(LB, 256, weight_right)
    t_ring(h + 3)
    t_ring(h + 1)
    g_far(z)

    poly(LB, 256, lS, lSP, lAP, lBP, lCP, lA, lambda rows, value: put(lRP, value, rows), lCT)

    t_in(col_of(h + 2, x), 0)
    t_in(col_of(h + 2, x), 1)
    t_spread(col_of(h + 2, x))
    g_ring(1 - z)

    def left_weight(index, carry):
        cols = pl.ds(pl.multiple_of(index * 256, 256), 256)
        lw = dot3(get(lRP), split(w_ref[:, cols]))
        put(QP, lw.T, cols)
        return carry

    lax.fori_loop(0, 4, left_weight, 0)

    t_rest(h)
    t_ring(h + 2)
    t_rest(h + 3)
    t_rest(h + 1)
    g_rest(1 - z)

    local_t.wait()
    local_g.wait()

    def add_chunks(pieces, start):
        def go(rows):
            total = None
            for k in pieces:
                part = dot(T[k, rows], Gr[k])
                total = part if total is None else total + part
            if start:
                gw[rows] = total
            else:
                gw[rows] += total

        rows_loop(LB, 256, go)

    t_rest(h + 2)

    def partner(yy, zz):
        far = row_of(yy, zz, 1 - c)
        g_in(far, 0)
        g_in(far, 1)
        return [row_of(yy, zz, c), far]

    add_chunks(partner(y, z) + partner(y + 3, z), True)
    add_chunks(partner(y + 1, z) + partner(y + 2, z), False)
    add_chunks(partner(y, 1 - z) + partner(y + 3, 1 - z), False)
    g_far(1 - z)
    add_chunks(partner(y + 1, 1 - z) + partner(y + 2, 1 - z), False)

    put(GWP, gw[...])

    def left_partial(index, carry):
        rows = pl.ds(pl.multiple_of(index * 128, 128), 128)
        lpart[index] = dot3(get(GWP, rows), get(MP), NT).reshape(2, 64, LB)
        return carry

    lax.fori_loop(0, 4, left_partial, 0)

    def rs_open(part, me, buf, sem, snd, plus, minus):
        far, nxt, prv = lax.rem(me + 2, 4), lax.rem(me + 1, 4), lax.rem(me + 3, 4)
        send(part(far, 0), buf.at[0], snd, sem.at[0], plus)
        send(part(far, 1), buf.at[1], snd, sem.at[1], minus)
        send(part(nxt, 1), buf.at[2], snd, sem.at[2], plus)
        send(part(prv, 0), buf.at[3], snd, sem.at[3], minus)

    def rs_mid(part, me, buf, stage, sem, snd, plus, minus):
        nxt, prv = lax.rem(me + 1, 4), lax.rem(me + 3, 4)
        arrive(buf.at[0], sem.at[0])
        stage[0] = buf[0] + part(nxt, 0)[...]
        arrive(buf.at[1], sem.at[1])
        stage[1] = buf[1] + part(prv, 1)[...]
        send(stage.at[0], buf.at[4], snd, sem.at[4], plus)
        send(stage.at[1], buf.at[5], snd, sem.at[5], minus)

    def rs_close(part, me, buf, sem):
        for index in range(2, 6):
            arrive(buf.at[index], sem.at[index])
        first = part(me, 0)[...] + (buf[3] + buf[4])
        second = part(me, 1)[...] + (buf[2] + buf[5])
        return first, second

    def ag_open(piece, me, sem, snd, plus, minus):
        for half in (0, 1):
            send(piece(me, half), piece(me, half), snd, sem.at[me, half], plus)
            send(piece(me, 1 - half), piece(me, 1 - half), snd, sem.at[me, 1 - half], minus)

    def ag_mid(piece, me, sem, snd, plus, minus):
        nxt, prv = lax.rem(me + 1, 4), lax.rem(me + 3, 4)
        arrive(piece(prv, 0), sem.at[prv, 0])
        send(piece(prv, 0), piece(prv, 0), snd, sem.at[prv, 0], plus)
        arrive(piece(nxt, 1), sem.at[nxt, 1])
        send(piece(nxt, 1), piece(nxt, 1), snd, sem.at[nxt, 1], minus)

    def ag_close(piece, me, sem):
        far, nxt, prv = lax.rem(me + 2, 4), lax.rem(me + 1, 4), lax.rem(me + 3, 4)
        for who, half in ((prv, 1), (nxt, 0), (far, 0), (far, 1)):
            arrive(piece(who, half), sem.at[who, half])

    def l_part(chunk, half):
        return lpart.at[chunk, half]

    def q_part(chunk, half):
        return Q.at[chunk, half]

    def z_piece(chunk, half):
        return Fx.at[x, chunk, half]

    def x_piece(chunk, half):
        return Fx.at[chunk, pl.ds(2 * half, 2)]

    def r_part(chunk, half):
        return rq.at[half, chunk]

    def y_piece(chunk, half):
        return Fy.at[chunk, half]

    rs_open(l_part, x, xr, xr_sem, ls, XP, XM)

    def right_partial(index, carry):
        cols = pl.ds(pl.multiple_of(index * RB, RB), RB)
        value = dot3(get(QP, cols), (gwh[:, cols], gwl[:, cols]))
        rpart[index // 2, index % 2] = value.reshape(4, 64, RB)
        return carry

    lax.fori_loop(0, 4, right_partial, 0)
    send(rpart.at[1 - c], rc, rs, rc_sem.at[0], CC)

    rs_mid(l_part, x, xr, xs, xr_sem, ls, XP, XM)
    arrive(rc, rc_sem.at[0])
    rq[...] = rpart[c] + rc[...]
    rs_open(r_part, y, yr, yr_sem, rs, YP, YM)

    first, second = rs_close(l_part, x, xr, xr_sem)
    Q[0:2] = first.reshape(2, 2, 16, LB)
    Q[2:4] = second.reshape(2, 2, 16, LB)
    rs_open(q_part, h, zr, zr_sem, ls, HP, HM)
    rs_mid(r_part, y, yr, ys, yr_sem, rs, YP, YM)
    rs_mid(q_part, h, zr, zs, zr_sem, ls, HP, HM)

    first, second = rs_close(r_part, y, yr, yr_sem)
    ro[0] = first
    ro[1] = second
    send(ro.at[1 - z], rz, rs, rz_sem.at[0], ZZ)

    first, second = rs_close(q_part, h, zr, zr_sem)
    Fx[x, h, 0] = first
    Fx[x, h, 1] = second
    ag_open(z_piece, h, za_sem, ls, HP, HM)

    arrive(rz, rz_sem.at[0])
    Fy[y] = (ro[z] + rz[...]).reshape(2, 32, RB)
    ag_open(y_piece, y, ya_sem, rs, YP, YM)

    ag_mid(z_piece, h, za_sem, ls, HP, HM)
    ag_mid(y_piece, y, ya_sem, rs, YP, YM)
    ag_close(z_piece, h, za_sem)
    ag_open(x_piece, x, xa_sem, ls, XP, XM)
    ag_close(y_piece, y, ya_sem)

    mine = 2 * c + z
    ea, aa, eb = rA.at[4], rA.at[5], rS.at[4]
    rS[5] = Fy[...].reshape(RB, RB)
    diff = adjoint(
        RB, RB, rS.at[5], at(rGP4(rsh, rsl), 4), at(rSP, mine), at(rAP, mine), at(rBP, mine), at(rCT, mine),
        at(rGP4(rah, ral), 4), ea, aa, eb,
    )
    nr_ref[mine] = updated(rp_ref[mine], diff, RB)
    ag_mid(x_piece, x, xa_sem, ls, XP, XM)
    send(nr_ref.at[mine], nr_ref.at[mine], rs, ra_sem.at[mine], ZZ)
    send(nr_ref.at[mine], nr_ref.at[mine], rs, ra_sem.at[mine], CC)
    ag_close(x_piece, x, xa_sem)
    across = 2 * c + 1 - z
    arrive(nr_ref.at[across], ra_sem.at[across])
    send(nr_ref.at[across], nr_ref.at[across], rs, ra_sem.at[across], CC)

    lw[...] = Fx[...].reshape(LB, LB)
    diff = adjoint(
        LB, 256, lw, lGP, lSP, lAP, lBP, lCT, lRP, gw.at[:, 0:LB], gw.at[:, LB : 2 * LB], lA,
    )
    nl_ref[...] = updated(lp_ref[...], diff, LB)

    for zz in (0, 1):
        block = 2 * (1 - c) + zz
        arrive(nr_ref.at[block], ra_sem.at[block])
    for copy in started:
        copy.wait_send()


def rGP4(first, second):
    return (first, second)


def pair_of(shape):
    return [pltpu.VMEM(shape, bf16)] * 2


def comm_call(tok, grad, weight, left_param, right_param):
    vm = pltpu.VMEM
    dma = pltpu.SemaphoreType.DMA
    left = (LB, LB)
    right = (6, RB, RB)
    scratch = [
        vm((16, 512, 256), bf16), vm((16, 256, 1024), bf16), vm((512, 1024), f32),
        *pair_of((512, 1024)), *pair_of((512, 1024)), *pair_of((1024, 512)), vm(left, f32),
        vm(left, f32), vm(left, f32), *pair_of(left), *pair_of(left), *pair_of(left), *pair_of(left), *pair_of(left),
        *pair_of(left), *pair_of(left),
        vm(right, f32), vm(right, f32), *pair_of(right), *pair_of(right), *pair_of(right), *pair_of(right),
        *pair_of(right), *pair_of(right),
        vm((4, 2, 64, LB), f32), vm((6, 64, LB), f32), vm((2, 64, LB), f32), vm((4, 2, 16, LB), f32),
        vm((6, 16, LB), f32), vm((2, 16, LB), f32), vm((4, 4, 2, 16, LB), f32),
        vm((2, 2, 4, 64, RB), f32), vm((2, 4, 64, RB), f32), vm((2, 4, 64, RB), f32), vm((6, 64, RB), f32),
        vm((2, 64, RB), f32), vm((2, 64, RB), f32), vm((64, RB), f32), vm((4, 2, 32, RB), f32),
        dma((16, 2)), dma((40,)), dma((16, 2)), dma((40,)), dma((3,)),
        dma((6,)), dma((6,)), dma((4, 2)), dma((4, 2)), dma((32,)),
        dma((1,)), dma((6,)), dma((1,)), dma((4, 2)), dma((4,)), dma((24,)),
    ]
    whole = pl.BlockSpec(memory_space=pltpu.VMEM)
    hbm = pl.BlockSpec(memory_space=pl.ANY)
    return pl.pallas_call(
        comm_kernel,
        out_shape=(jax.ShapeDtypeStruct(left, f32), jax.ShapeDtypeStruct((4, RB, RB), f32)),
        in_specs=[hbm, hbm, whole, whole, whole],
        out_specs=(whole, whole),
        scratch_shapes=scratch,
        compiler_params=pltpu.CompilerParams(
            collective_id=1, has_side_effects=True, vmem_limit_bytes=60 * 1024 * 1024
        ),
        name="comm",
    )(tok, grad, weight, left_param, right_param)


def final_kernel(
    w_ref, nl_ref, nr_ref, out_ref, nlo_ref, nro_ref,
    lS, lA, lsh, lsl, lah, lal, lbh, lbl, lch, lcl, lrh, lrl,
    rS, rA, rsh, rsl, rah, ral, rbh, rbl, rch, rcl, rrh, rrl,
):
    lSP, lAP, lBP, lCP, lRP = (lsh, lsl), (lah, lal), (lbh, lbl), (lch, lcl), (lrh, lrl)
    rSP, rAP, rBP, rCP, rRP = (rsh, rsl), (rah, ral), (rbh, rbl), (rch, rcl), (rrh, rrl)
    param = nl_ref[...]
    nlo_ref[...] = param
    s = (0.5 / math.sqrt(LB)) * (param - param.T)
    lS[...] = s
    put(lSP, s)
    poly(LB, 256, lS, lSP, lAP, lBP, lCP, lA, lambda rows, value: put(lRP, value, rows))

    def block(index, carry):
        param = nr_ref[index]
        nro_ref[index] = param
        s = (0.5 / math.sqrt(RB)) * (param - param.T)
        rS[...] = s
        put(rSP, s)
        poly(RB, RB, rS, rSP, rAP, rBP, rCP, rA, lambda rows, value: put(rRP, value, rows))
        cols = pl.ds(pl.multiple_of(index * RB, RB), RB)
        turned = dot3(get(lRP), split(w_ref[:, cols]))
        out_ref[:, cols] = dot3(split(turned), get(rRP))
        return carry

    lax.fori_loop(0, 4, block, 0)


def final_call(weight, new_left, new_right):
    vm = pltpu.VMEM
    left, right = (LB, LB), (RB, RB)
    whole = pl.BlockSpec(memory_space=pltpu.VMEM)
    scratch = [
        vm(left, f32), vm(left, f32), *pair_of(left), *pair_of(left), *pair_of(left), *pair_of(left), *pair_of(left),
        vm(right, f32), vm(right, f32), *pair_of(right), *pair_of(right), *pair_of(right), *pair_of(right),
        *pair_of(right),
    ]
    return pl.pallas_call(
        final_kernel,
        out_shape=(
            jax.ShapeDtypeStruct(weight.shape, f32), jax.ShapeDtypeStruct(left, f32),
            jax.ShapeDtypeStruct((4, RB, RB), f32),
        ),
        in_specs=[whole] * 3,
        out_specs=(whole,) * 3,
        scratch_shapes=scratch,
        compiler_params=pltpu.CompilerParams(vmem_limit_bytes=60 * 1024 * 1024),
        name="final",
    )(weight, new_left, new_right)


def body(tokens, grad_out, base_weight, left_param, right_param):
    left = left_param.reshape(LB, LB)
    new_left, new_right = comm_call(tokens.T, grad_out, base_weight, left, right_param)
    rotated, new_left, new_right = final_call(base_weight, new_left, new_right)
    return rotated, new_left.reshape(1, LB, LB), new_right


def solution(mesh):
    return jax.shard_map(
        body,
        mesh=mesh,
        in_specs=(
            P("col", "row"),
            P("row", "col"),
            P("row", "col"),
            P("row", None, None),
            P("col", None, None),
        ),
        out_specs=(P("row", "col"), P("row", None, None), P("col", None, None)),
        check_vma=False,
    )
```

time: 781 us -> 133 us (0.17)
  waiting for transfers between devices: 629 us -> 0 us
  Pallas kernels: 0 us -> 131 us
  matrix products: 95.5 us -> 0 us
  local copies, waits for them, and re-layouts: 25.2 us -> 1.79 us
  between operations: 16.4 us -> 0.64 us
  other arithmetic: 8.11 us -> 0 us
    psum x2 -> x0, waiting for transfers between devices: 282 us -> none  [the longest x1 163 us: body(): left_acc = lax.psum(partial_sum + placed, 'col')]
    all_gather x4 -> x0, waiting for transfers between devices: 185 us -> none  [the longest x1 55.2 us: body(): grads_all = lax.all_gather(grad_out, 'row', axis=0, tiled=True)]
    unnamed x8 -> x0, waiting for transfers between devices: 161 us -> none
    pallas_call x0 -> x2, Pallas kernels: none -> 131 us  [the longest x1 115 us: comm_call(): pl.pallas_call(comm_kernel, out_shape=(jax.ShapeDtypeStruct(left, f32), j...]
    dot_general x47 -> x0, matrix products: 95.5 us -> none  [the longest x42 71 us: batch_product(): return jnp.einsum('lab,lbc->lac', first, second, precision=precise)]
    unnamed x69 -> x1, local copies, waits for them, and re-layouts: 12.6 us -> 1.79 us
  transfers between devices with their start and end apart: 7 -> 0, of which waited for: 7 -> 0; matrix products, arithmetic and copies ran while one was open for 10% -> 0% of each run, Pallas kernels for 0% -> 0%
where the time goes in v1:
time: 133 us
  Pallas kernels  131 us (98%)
  local copies, waits for them, and re-layouts  1.79 us (1%)
    pallas_call x1, Pallas kernels, comm_call(): pl.pallas_call(comm_kernel, out_shape=(jax.ShapeDtypeStruct(left, f32), j...  115 us
    pallas_call x1, Pallas kernels, final_call(): pl.pallas_call(final_kernel, out_shape=(jax.ShapeDtypeStruct(weight.shape...  15.4 us

profile of v1, /device:TPU:32, one launch (start us, length us, event | category | flops | bytes accessed | tf_op | source)
XLA Modules:
  0.0 133.0 jit_solution(9080249141888608352)
XLA Ops:
  0.6 1.8 %copy.8 = bf16[256,512]{0,1:T(8,128)(2,1)} copy(bf16[256,512]{1,0:T(8,128)(2,1)} %param.5) | data formatting | bytes 524288 | tf_op args[0]
  2.4 115.2 %comm.1 = (f32[512,512]{1,0:T(8,128)}, f32[4,256,256]{2,1,0:T(8,128)}) custom-call(bf16[512,256]{1,0:T(8,128)(2,1)} %bitcast.4, bf16[256,1024]{1,0:T(8,128)(2,1)} %grad_ref.1, f32[512,1024]{1,0:T(8,128)} %w_ref.3, f32[512,512]{1,0:T(8,128)} %bitcast.3, f32[4,256,256]{2,1,0:T(8,128)} %rp_ref.1), custom_call_target="tpu_custom_call" | custom-call | tf_op jit(solution)/shard_map/comm/pallas_call | solution.py:530
  117.6 15.4 %final.1 = (f32[512,1024]{1,0:T(8,128)}, f32[512,512]{1,0:T(8,128)}, f32[4,256,256]{2,1,0:T(8,128)}) custom-call(f32[512,1024]{1,0:T(8,128)} %w_ref.3, f32[512,512]{1,0:T(8,128)} %get-tuple-element.8.nl_ref, f32[4,256,256]{2,1,0:T(8,128)} %get-tuple-element.9.nr_ref), custom_call_target="tpu_custom_call" | custom-call | tf_op jit(solution)/shard_map/final/pallas_call | solution.py:581

commit v2 on v1

v2 whole, which is shorter than its diff:
```python
import math

import jax
import jax.numpy as jnp
from jax import lax
from jax.experimental import pallas as pl
from jax.experimental.pallas import tpu as pltpu
from jax.sharding import PartitionSpec as P

step_rate = 0.3
epsilon = 1e-06
f32 = jnp.float32
bf16 = jnp.bfloat16
C2, C3, C4, C5, C6 = 1 / 2, 1 / 6, 1 / 24, 1 / 120, 1 / 720
LB, RB = 512, 256
NN = (((1,), (0,)), ((), ()))
NT = (((1,), (1,)), ((), ()))


def split(value):
    high = value.astype(bf16)
    return high, (value - high.astype(f32)).astype(bf16)


def put(pair, value, where=Ellipsis):
    pair[0][where], pair[1][where] = split(value)


def dot(first, second, dims=NN):
    return lax.dot_general(first, second, dims, preferred_element_type=f32)


def dot3(first, second, dims=NN):
    ah, al = first
    bh, bl = second
    return dot(ah, bh, dims) + (dot(ah, bl, dims) + dot(al, bh, dims))


def get(pair, where=Ellipsis):
    return pair[0][where], pair[1][where]


def rows_loop(total, tile, fn):
    def step(index, carry):
        fn(pl.ds(pl.multiple_of(index * tile, tile), tile))
        return carry

    lax.fori_loop(0, total // tile, step, 0)


def eye(rows, size):
    r = lax.broadcasted_iota(jnp.int32, (rows.size, size), 0) + rows.start
    c = lax.broadcasted_iota(jnp.int32, (rows.size, size), 1)
    return jnp.where(r == c, 1.0, 0.0).astype(f32)


def poly(size, tile, S, SP, AP, BP, CP, Af, finish, CT=None, pause=None):
    def square(rows):
        a = dot3(get(SP, rows), get(SP))
        Af[rows] = a
        put(AP, a, rows)

    rows_loop(size, tile, square)

    def cube(rows):
        b = dot3(get(SP, rows), get(AP))
        put(BP, b, rows)
        s = S[rows]
        a = Af[rows]
        even = C3 * eye(rows, size) + C5 * a
        odd = C4 * s + C6 * b
        put(CP, even + odd, rows)
        if CT is not None:
            put(CT, even - odd, rows)

    rows_loop(size, tile, cube)
    if pause is not None:
        pause()

    def last(rows):
        finish(rows, eye(rows, size) + S[rows] + C2 * Af[rows] + dot3(get(BP, rows), get(CP)))

    rows_loop(size, tile, last)


def adjoint(size, tile, G, GP, SP, AP, BP, CT, EP, Ea, Aa, Eb):
    def first(rows):
        c_bar = -dot3(get(BP, rows), get(GP))
        b_bar = dot3(get(GP, rows), get(CT)) + C6 * c_bar
        put(EP, b_bar, rows)
        g = G[rows]
        Ea[rows] = g + C4 * c_bar
        Aa[rows] = C2 * g + C5 * c_bar

    rows_loop(size, tile, first)
    return adjoint_end(size, tile, GP, SP, AP, EP, Ea, Aa, Eb)


def adjoint_end(size, tile, GP, SP, AP, EP, Ea, Aa, Eb):
    def second(rows):
        Ea[rows] += dot3(get(EP, rows), get(AP))
        Aa[rows] -= dot3(get(SP, rows), get(EP))

    rows_loop(size, tile, second)
    a_bar = Aa[...]
    put(GP, a_bar + a_bar.T)

    def third(rows):
        Eb[rows] = Ea[rows] - dot3(get(GP, rows), get(SP))

    rows_loop(size, tile, third)
    e = Eb[...]
    return e - e.T


def updated(param, diff, size):
    p = (0.5 / math.sqrt(size)) * diff
    mean = jnp.sum(p * p) * (1.0 / (size * size))
    return param - step_rate * p / jnp.sqrt(mean + epsilon)


def comm_kernel(
    tok_hbm, grad_ref, w_hbm, lp_hbm, rp_hbm, wrh_hbm, wrl_hbm, nl_hbm, nr_hbm,
    nl_ref, nr_ref, tok_v, w_ref, lp_ref, rp_ref,
    T, Gr, gw, gwh, gwl, mh, ml, qh, ql, lw,
    lS, lA, lsh, lsl, lah, lal, lbh, lbl, lch, lcl, lth, ltl, lrh, lrl, lgh, lgl,
    rS, rA, rsh, rsl, rah, ral, rbh, rbl, rch, rcl, rth, rtl, rrh, rrl,
    lpart, xr, xs, Q, zr, zs, Fx,
    rpart, rc, rq, yr, ys, ro, rz, Fy,
    t_recv, t_send, g_recv, g_send, loc_sem,
    xr_sem, zr_sem, za_sem, xa_sem, l_send,
    rc_sem, yr_sem, rz_sem, ya_sem, ra_sem, r_send,
):
    row = lax.axis_index("row")
    col = lax.axis_index("col")
    y, z, c = row // 4, (row // 2) % 2, row % 2
    h, x = col // 4, col % 4

    def row_of(yy, zz, cc):
        return (lax.rem(yy + 4, 4) * 2 + zz) * 2 + cc

    def col_of(hh, xx):
        return lax.rem(hh + 4, 4) * 4 + lax.rem(xx + 4, 4)

    YP, YM = {"row": row_of(y + 1, z, c)}, {"row": row_of(y + 3, z, c)}
    ZZ, CC = {"row": row_of(y, 1 - z, c)}, {"row": row_of(y, z, 1 - c)}
    XP, XM = {"col": col_of(h, x + 1)}, {"col": col_of(h, x + 3)}
    HP, HM = {"col": col_of(h + 1, x)}, {"col": col_of(h + 3, x)}
    started = []

    def send(src, dst, sems, recv, dev):
        counter = sems[1]
        copy = pltpu.make_async_remote_copy(
            src_ref=src, dst_ref=dst, send_sem=sems[0].at[counter[0]], recv_sem=recv,
            device_id=dev, device_id_type=pl.DeviceIdType.MESH,
        )
        counter[0] += 1
        copy.start()
        started.append(copy)

    def arrive(dst, recv):
        pltpu.make_async_remote_copy(
            src_ref=dst, dst_ref=dst, send_sem=loc_sem.at[5], recv_sem=recv,
            device_id=CC, device_id_type=pl.DeviceIdType.MESH,
        ).wait_recv()

    ts, gs, ls, rs = (t_send, [0]), (g_send, [0]), (l_send, [0]), (r_send, [0])

    load_tok = pltpu.make_async_copy(tok_hbm, tok_v, loc_sem.at[0])
    load_tok.start()
    barrier = pltpu.get_barrier_semaphore()
    for dev in (YP, YM, ZZ, CC, XP, XM, HP, HM):
        pl.semaphore_signal(barrier, inc=1, device_id=dev, device_id_type=pl.DeviceIdType.MESH)
    load_tok.wait()
    T[col] = tok_v[...].astype(f32).T.astype(bf16)
    pl.semaphore_wait(barrier, 8)

    def t_half(ref, half):
        return ref.at[pl.ds(256 * half, 256)]

    def g_half(ref, half):
        return ref.at[pl.ds(128 * half, 128)]

    def t_go(shard, half, dev):
        piece = t_half(T.at[shard], half)
        send(piece, piece, ts, t_recv.at[shard, half], dev)

    def t_in(shard, half):
        arrive(t_half(T.at[shard], half), t_recv.at[shard, half])

    def g_go(shard, half, dev, own=False):
        src = g_half(grad_ref if own else Gr.at[shard], half)
        send(src, g_half(Gr.at[shard], half), gs, g_recv.at[shard, half], dev)

    def g_in(shard, half):
        arrive(g_half(Gr.at[shard], half), g_recv.at[shard, half])

    for half in (0, 1):
        g_go(row, half, YP, True)
        g_go(row, 1 - half, YM, True)
        t_go(col, half, XP)
        t_go(col, 1 - half, XM)
        t_go(col, half, HP)
        t_go(col, 1 - half, HM)
    for half in (0, 1):
        g_go(row, half, ZZ, True)
    for half in (0, 1):
        g_go(row, half, CC, True)

    loads = [
        pltpu.make_async_copy(src, dst, loc_sem.at[1 + index])
        for index, (src, dst) in enumerate(
            ((rp_hbm, rp_ref), (lp_hbm, lp_ref), (w_hbm, w_ref), (grad_ref, Gr.at[row]))
        )
    ]
    for load in loads:
        load.start()

    def t_pass(shard, half, *devs):
        t_in(shard, half)
        for dev in devs:
            t_go(shard, half, dev)

    def g_pass(shard, half, *devs):
        g_in(shard, half)
        for dev in devs:
            g_go(shard, half, dev)
        g_go(shard, half, CC)

    lSP, lAP, lBP, lCP, lCT = (lsh, lsl), (lah, lal), (lbh, lbl), (lch, lcl), (lth, ltl)
    lRP, lGP = (lrh, lrl), (lgh, lgl)
    MP, QP, GWP = (mh, ml), (qh, ql), (gwh, gwl)

    def at(pair, index):
        return tuple(ref.at[index] for ref in pair)

    rSP, rAP, rBP, rCP, rCT = (rsh, rsl), (rah, ral), (rbh, rbl), (rch, rcl), (rth, rtl)
    rRP = (rrh, rrl)

    def right_one(index, carry, source=rp_ref, other=True):
        param = source[index]
        s = (0.5 / math.sqrt(RB)) * (param - param.T)
        rS[index] = s
        put(at(rSP, index), s)
        poly(
            RB, RB, rS.at[index], at(rSP, index), at(rAP, index), at(rBP, index), at(rCP, index), rA.at[index],
            lambda rows, value: put(at(rRP, index), value, rows), at(rCT, index) if other else None,
        )
        return carry

    def weight_right(rows):
        for index in range(4):
            cols = slice(RB * index, RB * (index + 1))
            m = dot3(split(w_ref[rows, cols]), get(at(rRP, index)))
            put(MP, m.T, (cols, rows))

    def left_weight(index, carry):
        cols = pl.ds(pl.multiple_of(index * 256, 256), 256)
        lw = dot3(get(lRP), split(w_ref[:, cols]))
        put(QP, lw.T, cols)
        return carry

    loads[0].wait()
    lax.fori_loop(0, 2, right_one, 0)
    t_pass(col_of(h, x + 3), 0, XP)
    t_pass(col_of(h, x + 1), 1, XM)
    lax.fori_loop(2, 4, right_one, 0)
    g_pass(row_of(y + 3, z, c), 0, YP)
    g_pass(row_of(y + 1, z, c), 1, YM)
    t_pass(col_of(h + 3, x), 0, XP, XM, HP)
    t_pass(col_of(h + 1, x), 1, XM, XP, HM)
    loads[2].wait()
    rows_loop(LB, 256, weight_right)
    t_pass(col_of(h + 3, x + 3), 0, XP)
    t_pass(col_of(h + 1, x + 1), 1, XM)
    g_pass(row_of(y + 3, z, c), 1)
    g_pass(row_of(y + 1, z, c), 0)
    t_pass(col_of(h + 3, x), 1, XP, XM)
    t_pass(col_of(h + 1, x), 0, XM, XP)
    loads[1].wait()
    param = lp_ref[...]
    s = (0.5 / math.sqrt(LB)) * (param - param.T)
    lS[...] = s
    put(lSP, s)
    other = row_of(y, 1 - z, c)

    def middle():
        t_pass(col_of(h + 3, x + 1), 1, XM)
        t_pass(col_of(h + 1, x + 3), 0, XP)
        g_pass(row_of(y + 2, z, c), 0)
        g_pass(row_of(y + 2, z, c), 1)
        g_pass(other, 0, YP, YM)

    poly(LB, 256, lS, lSP, lAP, lBP, lCP, lA, lambda rows, value: put(lRP, value, rows), lCT, middle)
    lax.fori_loop(0, 4, left_weight, 0)
    t_pass(col_of(h + 2, x), 0, XP, XM)
    t_pass(col_of(h + 2, x), 1, XM, XP)
    g_pass(other, 1, YM, YP)
    loads[3].wait()

    def add_chunks(pieces, start=False, end=False):
        def go(rows):
            total = None if start else gw[rows]
            for k in pieces:
                part = dot(T[k, rows], Gr[k])
                total = part if total is None else total + part
            if end:
                put(GWP, total, rows)
            else:
                gw[rows] = total

        rows_loop(LB, 256, go)

    def both(yy, zz):
        return [row_of(yy, zz, 0), row_of(yy, zz, 1)]

    def partner(yy, zz):
        far = row_of(yy, zz, 1 - c)
        g_in(far, 0)
        g_in(far, 1)

    def t_all(hh):
        for who in range(1, 4):
            for half in (0, 1):
                key = (hh, who, half)
                if key not in seen:
                    t_in(col_of(h + hh, x + who), half)

    seen = {
        (0, 3, 0), (0, 1, 1), (3, 3, 0), (1, 1, 1), (3, 1, 1), (1, 3, 0), (2, 3, 0), (2, 1, 1),
    }
    t_all(0)
    for yy in range(4):
        partner(y + yy, z)
    add_chunks(both(h, z), start=True)
    t_pass(col_of(h + 2, x + 3), 0, XP)
    t_pass(col_of(h + 2, x + 1), 1, XM)
    g_pass(row_of(y + 3, 1 - z, c), 0, YP)
    t_all(3)
    t_all(1)
    add_chunks(both(h + 1, z) + both(h + 3, z))
    g_pass(row_of(y + 1, 1 - z, c), 1, YM)
    g_pass(row_of(y + 1, 1 - z, c), 0)
    g_pass(row_of(y + 3, 1 - z, c), 1)
    t_all(2)
    partner(y, 1 - z)
    add_chunks(both(h + 2, z) + both(y, 1 - z))
    g_pass(row_of(y + 2, 1 - z, c), 0)
    partner(y + 1, 1 - z)
    partner(y + 3, 1 - z)
    add_chunks(both(y + 1, 1 - z) + both(y + 3, 1 - z))
    g_pass(row_of(y + 2, 1 - z, c), 1)
    partner(y + 2, 1 - z)
    add_chunks(both(y + 2, 1 - z), end=True)

    def rs_open(part, me, buf, sem, snd, plus, minus):
        far, nxt, prv = lax.rem(me + 2, 4), lax.rem(me + 1, 4), lax.rem(me + 3, 4)
        send(part(far, 0), buf.at[0], snd, sem.at[0], plus)
        send(part(far, 1), buf.at[1], snd, sem.at[1], minus)
        send(part(nxt, 1), buf.at[2], snd, sem.at[2], plus)
        send(part(prv, 0), buf.at[3], snd, sem.at[3], minus)

    def rs_mid(part, me, buf, stage, sem, snd, plus, minus):
        nxt, prv = lax.rem(me + 1, 4), lax.rem(me + 3, 4)
        arrive(buf.at[0], sem.at[0])
        stage[0] = buf[0] + part(nxt, 0)[...]
        send(stage.at[0], buf.at[4], snd, sem.at[4], plus)
        arrive(buf.at[1], sem.at[1])
        stage[1] = buf[1] + part(prv, 1)[...]
        send(stage.at[1], buf.at[5], snd, sem.at[5], minus)

    def rs_close(part, me, buf, sem):
        for index in range(2, 6):
            arrive(buf.at[index], sem.at[index])
        first = part(me, 0)[...] + (buf[3] + buf[4])
        second = part(me, 1)[...] + (buf[2] + buf[5])
        return first, second

    def ag_open(piece, me, sem, snd, plus, minus):
        for half in (0, 1):
            send(piece(me, half), piece(me, half), snd, sem.at[me, half], plus)
            send(piece(me, 1 - half), piece(me, 1 - half), snd, sem.at[me, 1 - half], minus)

    def ag_mid(piece, me, sem, snd, plus, minus):
        nxt, prv = lax.rem(me + 1, 4), lax.rem(me + 3, 4)
        arrive(piece(prv, 0), sem.at[prv, 0])
        send(piece(prv, 0), piece(prv, 0), snd, sem.at[prv, 0], plus)
        arrive(piece(nxt, 1), sem.at[nxt, 1])
        send(piece(nxt, 1), piece(nxt, 1), snd, sem.at[nxt, 1], minus)

    def ag_close(piece, me, sem):
        far, nxt, prv = lax.rem(me + 2, 4), lax.rem(me + 1, 4), lax.rem(me + 3, 4)
        for who, half in ((prv, 1), (nxt, 0), (far, 0), (far, 1)):
            arrive(piece(who, half), sem.at[who, half])

    class Left:
        def __init__(self, p):
            self.p = p
            self.part = lambda chunk, half: lpart.at[p, chunk, half]
            self.q = lambda chunk, half: Q.at[p, chunk, half]
            self.zp = lambda chunk, half: Fx.at[p, x, chunk, half]
            self.xp = lambda chunk, half: Fx.at[p, chunk, pl.ds(2 * half, 2)]

        def compute(self):
            cols = pl.ds(256 * self.p, 256)

            def go(index, carry):
                rows = pl.ds(pl.multiple_of(index * 256, 256), 256)
                value = dot3(get(GWP, rows), (mh[:, cols], ml[:, cols]))
                lpart[self.p, pl.ds(2 * index, 2)] = value.reshape(2, 2, 64, 256)
                return carry

            lax.fori_loop(0, 2, go, 0)

        def x_open(self):
            rs_open(self.part, x, xr.at[self.p], xr_sem.at[self.p], ls, XP, XM)

        def x_mid(self):
            rs_mid(self.part, x, xr.at[self.p], xs.at[self.p], xr_sem.at[self.p], ls, XP, XM)

        def z_open(self):
            p = self.p
            first, second = rs_close(self.part, x, xr.at[p], xr_sem.at[p])
            Q[p, 0:2] = first.reshape(2, 2, 16, 256)
            Q[p, 2:4] = second.reshape(2, 2, 16, 256)
            rs_open(self.q, h, zr.at[p], zr_sem.at[p], ls, HP, HM)

        def z_mid(self):
            p = self.p
            rs_mid(self.q, h, zr.at[p], zs.at[p], zr_sem.at[p], ls, HP, HM)

        def za_open(self):
            p = self.p
            first, second = rs_close(self.q, h, zr.at[p], zr_sem.at[p])
            Fx[p, x, h, 0] = first
            Fx[p, x, h, 1] = second
            ag_open(self.zp, h, za_sem.at[p], ls, HP, HM)

        def za_mid(self):
            ag_mid(self.zp, h, za_sem.at[self.p], ls, HP, HM)

        def xa_open(self):
            ag_close(self.zp, h, za_sem.at[self.p])
            ag_open(self.xp, x, xa_sem.at[self.p], ls, XP, XM)

        def xa_mid(self):
            ag_mid(self.xp, x, xa_sem.at[self.p], ls, XP, XM)

        def finish(self):
            p = self.p
            ag_close(self.xp, x, xa_sem.at[p])
            value = Fx[p].reshape(LB, 256)
            cols = slice(256 * p, 256 * (p + 1))
            pair = split(value)
            lgh[...], lgl[...] = pair

            def go(index, carry):
                rows = pl.ds(pl.multiple_of(index * 256, 256), 256)
                lA[rows, cols] = -dot3(get(lBP, rows), get(lGP))
                part = dot3(get(lGP, rows), get(lCT, cols))
                lw[rows] = part if p == 0 else lw[rows] + part
                return carry

            lax.fori_loop(0, 2, go, 0)

    def r_part(chunk, half):
        return rq.at[half, chunk]

    def y_piece(chunk, half):
        return Fy.at[chunk, half]

    L0, L1 = Left(0), Left(1)

    def right_partial(index):
        cols = pl.ds(pl.multiple_of(index * RB, RB), RB)
        value = dot3(get(QP, cols), (gwh[:, cols], gwl[:, cols]))
        rpart[index // 2, index % 2] = value.reshape(4, 64, RB)

    L0.compute()
    L0.x_open()
    L1.compute()
    right_partial(2 * (1 - c))
    right_partial(2 * (1 - c) + 1)
    send(rpart.at[1 - c], rc, rs, rc_sem.at[0], CC)
    L0.x_mid()
    L1.x_open()
    right_partial(2 * c)
    right_partial(2 * c + 1)
    arrive(rc, rc_sem.at[0])
    rq[...] = rpart[c] + rc[...]
    rs_open(r_part, y, yr, yr_sem, rs, YP, YM)
    L0.z_open()
    L1.x_mid()
    rs_mid(r_part, y, yr, ys, yr_sem, rs, YP, YM)
    L0.z_mid()
    L1.z_open()
    first, second = rs_close(r_part, y, yr, yr_sem)
    ro[0] = first
    ro[1] = second
    send(ro, rz, rs, rz_sem.at[0], ZZ)
    L0.za_open()
    L1.z_mid()
    arrive(rz, rz_sem.at[0])
    Fy[y] = ro[...] + rz[...]
    ag_open(y_piece, y, ya_sem, rs, YP, YM)
    L0.za_mid()
    L1.za_open()
    ag_mid(y_piece, y, ya_sem, rs, YP, YM)
    L0.xa_open()
    L1.za_mid()
    ag_close(y_piece, y, ya_sem)

    def right_new(zz):
        mine = 2 * c + zz
        rS[5] = Fy[:, zz].reshape(RB, RB)
        put(at(rSP, 4), rS[5])
        diff = adjoint(
            RB, RB, rS.at[5], at(rSP, 4), at(rSP, mine), at(rAP, mine), at(rBP, mine), at(rCT, mine),
            at(rAP, 4), rA.at[4], rA.at[5], rS.at[4],
        )
        nr_ref[mine] = updated(rp_ref[mine], diff, RB)
        send(nr_ref.at[mine], nr_ref.at[mine], rs, ra_sem.at[mine], CC)

    def turn_right(index):
        right_one(index, 0, nr_ref, False)
        cols = pl.ds(pl.multiple_of(index * RB, RB), RB)

        def go(rows):
            gwh[rows, cols], gwl[rows, cols] = split(dot3(split(w_ref[rows, cols]), get(at(rRP, index))))

        rows_loop(LB, 256, go)

    def turn_other(zz):
        index = 2 * (1 - c) + zz
        arrive(nr_ref.at[index], ra_sem.at[index])
        turn_right(index)

    right_new(0)
    L0.xa_mid()
    right_new(1)
    L1.xa_open()
    turn_right(2 * c)
    L0.finish()
    turn_other(0)
    L1.xa_mid()
    turn_right(2 * c + 1)
    turn_other(1)
    outs = [
        pltpu.make_async_copy(src, dst, loc_sem.at[1 + index])
        for index, (src, dst) in enumerate(((nr_ref, nr_hbm), (gwh, wrh_hbm), (gwl, wrl_hbm)))
    ]
    for copy in outs:
        copy.start()
    L1.finish()

    Ea, Aa = gw.at[:, 0:LB], gw.at[:, LB : 2 * LB]

    def join(rows):
        c_bar = lA[rows]
        g = jnp.concatenate([Fx[0, pl.ds(2 * (rows.start // 256), 2)].reshape(256, 256),
                             Fx[1, pl.ds(2 * (rows.start // 256), 2)].reshape(256, 256)], axis=1)
        put(lRP, lw[rows] + C6 * c_bar, rows)
        Ea[rows] = g + C4 * c_bar
        Aa[rows] = C2 * g + C5 * c_bar

    join(pl.ds(0, 256))
    join(pl.ds(256, 256))
    diff = adjoint_end(LB, 256, lCP, lSP, lAP, lRP, Ea, Aa, lA)
    nl_ref[...] = updated(lp_ref[...], diff, LB)
    put_left = pltpu.make_async_copy(nl_ref, nl_hbm, loc_sem.at[0])
    put_left.start()

    for copy in started:
        copy.wait_send()
    for copy in [put_left] + outs:
        copy.wait()


def pair_of(shape):
    return [pltpu.VMEM(shape, bf16)] * 2


def comm_call(tok, grad, weight, left_param, right_param):
    vm = pltpu.VMEM
    dma = pltpu.SemaphoreType.DMA
    left = (LB, LB)
    right = (6, RB, RB)
    scratch = [
        vm(left, f32), vm((4, RB, RB), f32), vm((256, 512), bf16), vm((512, 1024), f32), vm(left, f32),
        vm((4, RB, RB), f32),
        vm((16, 512, 256), bf16), vm((16, 256, 1024), bf16), vm((512, 1024), f32),
        *pair_of((512, 1024)), *pair_of((1024, 512)), *pair_of((1024, 512)), vm(left, f32),
        vm(left, f32), vm(left, f32), *pair_of(left), *pair_of(left), *pair_of(left), *pair_of(left), *pair_of(left),
        *pair_of(left), *pair_of((512, 256)),
        vm(right, f32), vm(right, f32), *pair_of(right), *pair_of(right), *pair_of(right), *pair_of(right),
        *pair_of(right), *pair_of(right),
        vm((2, 4, 2, 64, 256), f32), vm((2, 6, 64, 256), f32), vm((2, 2, 64, 256), f32), vm((2, 4, 2, 16, 256), f32),
        vm((2, 6, 16, 256), f32), vm((2, 2, 16, 256), f32), vm((2, 4, 4, 2, 16, 256), f32),
        vm((2, 2, 4, 64, RB), f32), vm((2, 4, 64, RB), f32), vm((2, 4, 64, RB), f32), vm((6, 64, RB), f32),
        vm((2, 64, RB), f32), vm((2, 64, RB), f32), vm((2, 64, RB), f32), vm((4, 2, 64, RB), f32),
        dma((16, 2)), dma((30,)), dma((16, 2)), dma((30,)), dma((6,)),
        dma((2, 6)), dma((2, 6)), dma((2, 4, 2)), dma((2, 4, 2)), dma((48,)),
        dma((1,)), dma((6,)), dma((1,)), dma((4, 2)), dma((4,)), dma((24,)),
    ]
    hbm = pl.BlockSpec(memory_space=pl.ANY)
    return pl.pallas_call(
        comm_kernel,
        out_shape=(
            jax.ShapeDtypeStruct(weight.shape, bf16), jax.ShapeDtypeStruct(weight.shape, bf16),
            jax.ShapeDtypeStruct(left, f32),
            jax.ShapeDtypeStruct((4, RB, RB), f32),
        ),
        in_specs=[hbm] * 5,
        out_specs=(hbm,) * 4,
        scratch_shapes=scratch,
        compiler_params=pltpu.CompilerParams(
            collective_id=1, has_side_effects=True, vmem_limit_bytes=60 * 1024 * 1024
        ),
        name="comm",
    )(tok, grad, weight, left_param, right_param)


def final_kernel(
    wrh, wrl, nl, nr, out, nlo, nro, wh, wl, acc, nl_v, nr_v, S, A, sh, sl, ah, al, bh, bl, ch, cl, rh, rl, sem
):
    def copy(src, dst, index):
        made = pltpu.make_async_copy(src, dst, sem.at[index])
        made.start()
        return made

    left_in = copy(nl, nl_v, 0)
    right_in = copy(nr, nr_v, 1)
    weight_in = [copy(wrh, wh, 2), copy(wrl, wl, 3)]
    left_in.wait()
    outs = [copy(nl_v, nlo, 4)]
    param = nl_v[...]
    s = (0.5 / math.sqrt(LB)) * (param - param.T)
    S[...] = s
    put((sh, sl), s)
    right_in.wait()
    outs.append(copy(nr_v, nro, 5))
    poly(
        LB, 256, S, (sh, sl), (ah, al), (bh, bl), (ch, cl), A, lambda rows, value: put((rh, rl), value, rows)
    )
    for made in weight_in:
        made.wait()
    for index in range(4):
        cols = pl.ds(256 * index, 256)
        acc[:, cols] = dot3((rh[...], rl[...]), (wh[:, cols], wl[:, cols]))
        outs.append(copy(acc.at[:, cols], out.at[:, cols], 6 + index))
    for made in outs:
        made.wait()


def final_call(wrh, wrl, new_left, new_right):
    vm = pltpu.VMEM
    hbm = pl.BlockSpec(memory_space=pl.ANY)
    left = (LB, LB)
    return pl.pallas_call(
        final_kernel,
        out_shape=(
            jax.ShapeDtypeStruct(wrh.shape, f32), jax.ShapeDtypeStruct(left, f32),
            jax.ShapeDtypeStruct((4, RB, RB), f32),
        ),
        in_specs=[hbm] * 4,
        out_specs=(hbm,) * 3,
        scratch_shapes=[
            *pair_of(wrh.shape), vm(wrh.shape, f32), vm(left, f32), vm((4, RB, RB), f32), vm(left, f32), vm(left, f32),
            *pair_of(left), *pair_of(left), *pair_of(left), *pair_of(left), *pair_of(left),
            pltpu.SemaphoreType.DMA((10,)),
        ],
        compiler_params=pltpu.CompilerParams(vmem_limit_bytes=60 * 1024 * 1024),
        name="final",
    )(wrh, wrl, new_left, new_right)


def body(tokens, grad_out, base_weight, left_param, right_param):
    left = left_param.reshape(LB, LB)
    given = comm_call(tokens, grad_out, base_weight, left, right_param)
    rotated, new_left, new_right = final_call(*given)
    return rotated, new_left.reshape(1, LB, LB), new_right


def solution(mesh):
    return jax.shard_map(
        body,
        mesh=mesh,
        in_specs=(
            P("col", "row"),
            P("row", "col"),
            P("row", "col"),
            P("row", None, None),
            P("col", None, None),
        ),
        out_specs=(P("row", "col"), P("row", None, None), P("col", None, None)),
        check_vma=False,
    )
```

time: 133 us -> 115 us (0.86)
  Pallas kernels: 131 us -> 114 us
  local copies, waits for them, and re-layouts: 1.79 us -> 0 us
    pallas_call x2, Pallas kernels: 131 us -> 114 us  [the longest x1 105 us: comm_call(): pl.pallas_call(comm_kernel, out_shape=(jax.ShapeDtypeStruct(weight.shape,...]
    unnamed x1 -> x0, local copies, waits for them, and re-layouts: 1.79 us -> none
where the time goes in v2:
time: 115 us
  Pallas kernels  114 us (99%)
    pallas_call x1, Pallas kernels, comm_call(): pl.pallas_call(comm_kernel, out_shape=(jax.ShapeDtypeStruct(weight.shape,...  105 us
    pallas_call x1, Pallas kernels, final_call(): pl.pallas_call(final_kernel, out_shape=(jax.ShapeDtypeStruct(wrh.shape, f...  8.4 us

profile of v2, /device:TPU:32, one launch (start us, length us, event | category | flops | bytes accessed | tf_op | source)
XLA Modules:
  0.0 114.5 jit_solution(11204124432189711669)
XLA Ops:
  0.6 105.3 %comm.1 = (bf16[512,1024]{1,0:T(8,128)(2,1)}, bf16[512,1024]{1,0:T(8,128)(2,1)}, f32[512,512]{1,0:T(8,128)}, f32[4,256,256]{2,1,0:T(8,128)}) custom-call(bf16[256,512]{1,0:T(8,128)(2,1)} %tok_hbm.1, bf16[256,1024]{1,0:T(8,128)(2,1)} %grad_ref.1, f32[512,1024]{1,0:T(8,128)} %w_hbm.1, f32[512,512]{1,0:T(8,128)} %bitcast.2, f32[4,256,256]{2,1,0:T(8,128)} %rp_hbm.1), custom_call_target="tpu_custom_call" | custom-call | tf_op jit(solution)/shard_map/comm/pallas_call | solution.py:606
  106.0 8.4 %final.1 = (f32[512,1024]{1,0:T(8,128)}, f32[512,512]{1,0:T(8,128)}, f32[4,256,256]{2,1,0:T(8,128)}) custom-call(bf16[512,1024]{1,0:T(8,128)(2,1)} %get-tuple-element.10.wrh, bf16[512,1024]{1,0:T(8,128)(2,1)} %get-tuple-element.11.wrl, f32[512,512]{1,0:T(8,128)} %get-tuple-element.12.nl, f32[4,256,256]{2,1,0:T(8,128)} %get-tuple-element.13.nr), custom_call_target="tpu_custom_call" | custom-call | tf_op jit(solution)/shard_map/final/pallas_call | solution.py:659

commit v3 on v2

--- a/solution.py
+++ b/solution.py
@@ -54,13 +54,15 @@
     return jnp.where(r == c, 1.0, 0.0).astype(f32)
 
 
-def poly(size, tile, S, SP, AP, BP, CP, Af, finish, CT=None, pause=None):
+def poly(size, tile, S, SP, AP, BP, CP, Af, finish, CT=None, pause=None, early=None):
     def square(rows):
         a = dot3(get(SP, rows), get(SP))
         Af[rows] = a
         put(AP, a, rows)
 
     rows_loop(size, tile, square)
+    if early is not None:
+        early()
 
     def cube(rows):
         b = dot3(get(SP, rows), get(AP))
@@ -120,16 +122,16 @@
 
 
 def comm_kernel(
-    tok_hbm, grad_ref, w_hbm, lp_hbm, rp_hbm, wrh_hbm, wrl_hbm, nl_hbm, nr_hbm,
-    nl_ref, nr_ref, tok_v, w_ref, lp_ref, rp_ref,
-    T, Gr, gw, gwh, gwl, mh, ml, qh, ql, lw,
+    tok_hbm, grad_ref, w_hbm, lp_hbm, rp_hbm, gwh, gwl, nl_ref, nr_hbm,
+    nr_ref, tok_v, w_ref, lp_ref, rp_ref,
+    T, Gr, gw, mh, ml, qh, ql,
     lS, lA, lsh, lsl, lah, lal, lbh, lbl, lch, lcl, lth, ltl, lrh, lrl, lgh, lgl,
     rS, rA, rsh, rsl, rah, ral, rbh, rbl, rch, rcl, rth, rtl, rrh, rrl,
     lpart, xr, xs, Q, zr, zs, Fx,
     rpart, rc, rq, yr, ys, ro, rz, Fy,
     t_recv, t_send, g_recv, g_send, loc_sem,
     xr_sem, zr_sem, za_sem, xa_sem, l_send,
-    rc_sem, yr_sem, rz_sem, ya_sem, ra_sem, r_send,
+    rc_sem, yr_sem, rz_sem, ya_sem, ra_sem, rb_sem, r_send,
 ):
     row = lax.axis_index("row")
     col = lax.axis_index("col")
@@ -179,7 +181,7 @@
         return ref.at[pl.ds(256 * half, 256)]
 
     def g_half(ref, half):
-        return ref.at[pl.ds(128 * half, 128)]
+        return ref.at[pl.ds(64 * half, 64)]
 
     def t_go(shard, half, dev):
         piece = t_half(T.at[shard], half)
@@ -196,16 +198,17 @@
         arrive(g_half(Gr.at[shard], half), g_recv.at[shard, half])
 
     for half in (0, 1):
-        g_go(row, half, YP, True)
-        g_go(row, 1 - half, YM, True)
         t_go(col, half, XP)
         t_go(col, 1 - half, XM)
         t_go(col, half, HP)
         t_go(col, 1 - half, HM)
-    for half in (0, 1):
-        g_go(row, half, ZZ, True)
-    for half in (0, 1):
-        g_go(row, half, CC, True)
+    for q in range(4):
+        g_go(row, q, YP, True)
+        g_go(row, (q + 2) % 4, YM, True)
+    for q in (0, 2, 1):
+        g_go(row, q, ZZ, True)
+    for q in range(4):
+        g_go(row, q, CC, True)
 
     loads = [
         pltpu.make_async_copy(src, dst, loc_sem.at[1 + index])
@@ -243,7 +246,7 @@
         rS[index] = s
         put(at(rSP, index), s)
         poly(
-            RB, RB, rS.at[index], at(rSP, index), at(rAP, index), at(rBP, index), at(rCP, index), rA.at[index],
+            RB, RB, rS.at[index], at(rSP, index), at(rAP, index), at(rBP, index), at(rCP, 0), rA.at[index],
             lambda rows, value: put(at(rRP, index), value, rows), at(rCT, index) if other else None,
         )
         return carry
@@ -260,42 +263,63 @@
         put(QP, lw.T, cols)
         return carry
 
+    up, down, far = y + 1, y + 3, y + 2
+    other = row_of(y, 1 - z, c)
+
+    def g_up(q, zz, *devs):
+        g_pass(row_of(up, zz, c), q, *devs)
+
+    def g_down(q, zz, *devs):
+        g_pass(row_of(down, zz, c), q, *devs)
+
+    def g_far(q, zz):
+        g_pass(row_of(far, zz, c), q)
+
     loads[0].wait()
-    lax.fori_loop(0, 2, right_one, 0)
+    lax.fori_loop(0, 4, right_one, 0)
     t_pass(col_of(h, x + 3), 0, XP)
     t_pass(col_of(h, x + 1), 1, XM)
-    lax.fori_loop(2, 4, right_one, 0)
-    g_pass(row_of(y + 3, z, c), 0, YP)
-    g_pass(row_of(y + 1, z, c), 1, YM)
+    g_down(0, z, YP)
+    g_up(2, z, YM)
+    loads[2].wait()
+    weight_right(pl.ds(0, 256))
+    g_down(1, z, YP)
+    g_up(3, z, YM)
     t_pass(col_of(h + 3, x), 0, XP, XM, HP)
     t_pass(col_of(h + 1, x), 1, XM, XP, HM)
-    loads[2].wait()
-    rows_loop(LB, 256, weight_right)
-    t_pass(col_of(h + 3, x + 3), 0, XP)
-    t_pass(col_of(h + 1, x + 1), 1, XM)
-    g_pass(row_of(y + 3, z, c), 1)
-    g_pass(row_of(y + 1, z, c), 0)
-    t_pass(col_of(h + 3, x), 1, XP, XM)
-    t_pass(col_of(h + 1, x), 0, XM, XP)
+    g_go(row, 3, ZZ, True)
+    weight_right(pl.ds(256, 256))
     loads[1].wait()
     param = lp_ref[...]
     s = (0.5 / math.sqrt(LB)) * (param - param.T)
     lS[...] = s
     put(lSP, s)
-    other = row_of(y, 1 - z, c)
+    g_down(2, z)
+    g_up(0, z)
+
+    def early():
+        g_down(3, z)
+        g_up(1, z)
+        t_pass(col_of(h + 3, x + 3), 0, XP)
+        t_pass(col_of(h + 1, x + 1), 1, XM)
+        t_pass(col_of(h + 3, x), 1, XM, XP)
+        t_pass(col_of(h + 1, x), 0, XP, XM)
 
     def middle():
-        t_pass(col_of(h + 3, x + 1), 1, XM)
-        t_pass(col_of(h + 1, x + 3), 0, XP)
-        g_pass(row_of(y + 2, z, c), 0)
-        g_pass(row_of(y + 2, z, c), 1)
+        g_far(0, z)
+        g_far(2, z)
         g_pass(other, 0, YP, YM)
 
-    poly(LB, 256, lS, lSP, lAP, lBP, lCP, lA, lambda rows, value: put(lRP, value, rows), lCT, middle)
+    poly(LB, 256, lS, lSP, lAP, lBP, lCP, lA, lambda rows, value: put(lRP, value, rows), lCT, middle, early)
+    g_far(1, z)
+    g_far(3, z)
+    g_pass(other, 2, YM, YP)
     lax.fori_loop(0, 4, left_weight, 0)
-    t_pass(col_of(h + 2, x), 0, XP, XM)
-    t_pass(col_of(h + 2, x), 1, XM, XP)
-    g_pass(other, 1, YM, YP)
+    g_down(0, 1 - z, YP)
+    g_pass(other, 1, YP, YM)
+    t_pass(col_of(h + 3, x + 1), 1, XM)
+    t_pass(col_of(h + 1, x + 3), 0, XP)
+    g_up(2, 1 - z, YM)
     loads[3].wait()
 
     def add_chunks(pieces, start=False, end=False):
@@ -316,8 +340,8 @@
 
     def partner(yy, zz):
         far = row_of(yy, zz, 1 - c)
-        g_in(far, 0)
-        g_in(far, 1)
+        for q in range(4):
+            g_in(far, q)
 
     def t_all(hh):
         for who in range(1, 4):
@@ -333,30 +357,41 @@
     for yy in range(4):
         partner(y + yy, z)
     add_chunks(both(h, z), start=True)
+    t_pass(col_of(h + 2, x), 0, XP, XM)
+    t_pass(col_of(h + 2, x), 1, XM, XP)
+    g_down(1, 1 - z, YP)
+    t_all(3)
+    t_all(1)
+    add_chunks(both(h + 1, z))
+    g_pass(other, 3, YM, YP)
+    g_up(0, 1 - z)
+    g_down(2, 1 - z)
+    add_chunks(both(h + 3, z))
     t_pass(col_of(h + 2, x + 3), 0, XP)
     t_pass(col_of(h + 2, x + 1), 1, XM)
-    g_pass(row_of(y + 3, 1 - z, c), 0, YP)
-    t_all(3)
-    t_all(1)
-    add_chunks(both(h + 1, z) + both(h + 3, z))
-    g_pass(row_of(y + 1, 1 - z, c), 1, YM)
-    g_pass(row_of(y + 1, 1 - z, c), 0)
-    g_pass(row_of(y + 3, 1 - z, c), 1)
+    g_up(1, 1 - z)
+    g_far(0, 1 - z)
+    g_far(2, 1 - z)
+    g_up(3, 1 - z, YM)
+    g_down(3, 1 - z)
+    g_far(1, 1 - z)
     t_all(2)
     partner(y, 1 - z)
     add_chunks(both(h + 2, z) + both(y, 1 - z))
-    g_pass(row_of(y + 2, 1 - z, c), 0)
     partner(y + 1, 1 - z)
     partner(y + 3, 1 - z)
     add_chunks(both(y + 1, 1 - z) + both(y + 3, 1 - z))
-    g_pass(row_of(y + 2, 1 - z, c), 1)
+    g_far(3, 1 - z)
     partner(y + 2, 1 - z)
     add_chunks(both(y + 2, 1 - z), end=True)
 
     def rs_open(part, me, buf, sem, snd, plus, minus):
-        far, nxt, prv = lax.rem(me + 2, 4), lax.rem(me + 1, 4), lax.rem(me + 3, 4)
+        far = lax.rem(me + 2, 4)
         send(part(far, 0), buf.at[0], snd, sem.at[0], plus)
         send(part(far, 1), buf.at[1], snd, sem.at[1], minus)
+
+    def rs_single(part, me, buf, sem, snd, plus, minus):
+        nxt, prv = lax.rem(me + 1, 4), lax.rem(me + 3, 4)
         send(part(nxt, 1), buf.at[2], snd, sem.at[2], plus)
         send(part(prv, 0), buf.at[3], snd, sem.at[3], minus)
 
@@ -415,6 +450,9 @@
         def x_open(self):
             rs_open(self.part, x, xr.at[self.p], xr_sem.at[self.p], ls, XP, XM)
 
+        def x_single(self):
+            rs_single(self.part, x, xr.at[self.p], xr_sem.at[self.p], ls, XP, XM)
+
         def x_mid(self):
             rs_mid(self.part, x, xr.at[self.p], xs.at[self.p], xr_sem.at[self.p], ls, XP, XM)
 
@@ -424,6 +462,7 @@
             Q[p, 0:2] = first.reshape(2, 2, 16, 256)
             Q[p, 2:4] = second.reshape(2, 2, 16, 256)
             rs_open(self.q, h, zr.at[p], zr_sem.at[p], ls, HP, HM)
+            rs_single(self.q, h, zr.at[p], zr_sem.at[p], ls, HP, HM)
 
         def z_mid(self):
             p = self.p
@@ -469,6 +508,7 @@
     def y_piece(chunk, half):
         return Fy.at[chunk, half]
 
+    lw = gw.at[:, LB : 2 * LB]
     L0, L1 = Left(0), Left(1)
 
     def right_partial(index):
@@ -479,35 +519,39 @@
     L0.compute()
     L0.x_open()
     L1.compute()
+    L1.x_open()
+    L0.x_single()
     right_partial(2 * (1 - c))
     right_partial(2 * (1 - c) + 1)
     send(rpart.at[1 - c], rc, rs, rc_sem.at[0], CC)
-    L0.x_mid()
-    L1.x_open()
     right_partial(2 * c)
     right_partial(2 * c + 1)
+    L0.x_mid()
+    L1.x_single()
     arrive(rc, rc_sem.at[0])
     rq[...] = rpart[c] + rc[...]
     rs_open(r_part, y, yr, yr_sem, rs, YP, YM)
+    rs_single(r_part, y, yr, yr_sem, rs, YP, YM)
+    L1.x_mid()
     L0.z_open()
-    L1.x_mid()
     rs_mid(r_part, y, yr, ys, yr_sem, rs, YP, YM)
+    L1.z_open()
     L0.z_mid()
-    L1.z_open()
     first, second = rs_close(r_part, y, yr, yr_sem)
     ro[0] = first
     ro[1] = second
     send(ro, rz, rs, rz_sem.at[0], ZZ)
+    L1.z_mid()
     L0.za_open()
-    L1.z_mid()
+    L1.za_open()
     arrive(rz, rz_sem.at[0])
     Fy[y] = ro[...] + rz[...]
     ag_open(y_piece, y, ya_sem, rs, YP, YM)
     L0.za_mid()
-    L1.za_open()
+    L1.za_mid()
     ag_mid(y_piece, y, ya_sem, rs, YP, YM)
     L0.xa_open()
-    L1.za_mid()
+    L1.xa_open()
     ag_close(y_piece, y, ya_sem)
 
     def right_new(zz):
@@ -521,8 +565,13 @@
         nr_ref[mine] = updated(rp_ref[mine], diff, RB)
         send(nr_ref.at[mine], nr_ref.at[mine], rs, ra_sem.at[mine], CC)
 
+    def new_rotation(zz):
+        mine = 2 * c + zz
+        right_one(mine, 0, nr_ref, False)
+        send(rrh.at[mine], rrh.at[mine], rs, rb_sem.at[mine, 0], CC)
+        send(rrl.at[mine], rrl.at[mine], rs, rb_sem.at[mine, 1], CC)
+
     def turn_right(index):
-        right_one(index, 0, nr_ref, False)
         cols = pl.ds(pl.multiple_of(index * RB, RB), RB)
 
         def go(rows):
@@ -532,25 +581,25 @@
 
     def turn_other(zz):
         index = 2 * (1 - c) + zz
-        arrive(nr_ref.at[index], ra_sem.at[index])
+        arrive(rrh.at[index], rb_sem.at[index, 0])
+        arrive(rrl.at[index], rb_sem.at[index, 1])
         turn_right(index)
 
     right_new(0)
     L0.xa_mid()
     right_new(1)
-    L1.xa_open()
+    new_rotation(0)
+    new_rotation(1)
+    L1.xa_mid()
     turn_right(2 * c)
+    turn_right(2 * c + 1)
     L0.finish()
     turn_other(0)
-    L1.xa_mid()
-    turn_right(2 * c + 1)
     turn_other(1)
-    outs = [
-        pltpu.make_async_copy(src, dst, loc_sem.at[1 + index])
-        for index, (src, dst) in enumerate(((nr_ref, nr_hbm), (gwh, wrh_hbm), (gwl, wrl_hbm)))
-    ]
-    for copy in outs:
-        copy.start()
+    for zz in (0, 1):
+        arrive(nr_ref.at[2 * (1 - c) + zz], ra_sem.at[2 * (1 - c) + zz])
+    put_right = pltpu.make_async_copy(nr_ref, nr_hbm, loc_sem.at[0])
+    put_right.start()
     L1.finish()
 
     Ea, Aa = gw.at[:, 0:LB], gw.at[:, LB : 2 * LB]
@@ -567,13 +616,10 @@
     join(pl.ds(256, 256))
     diff = adjoint_end(LB, 256, lCP, lSP, lAP, lRP, Ea, Aa, lA)
     nl_ref[...] = updated(lp_ref[...], diff, LB)
-    put_left = pltpu.make_async_copy(nl_ref, nl_hbm, loc_sem.at[0])
-    put_left.start()
 
     for copy in started:
         copy.wait_send()
-    for copy in [put_left] + outs:
-        copy.wait()
+    put_right.wait()
 
 
 def pair_of(shape):
@@ -586,23 +632,24 @@
     left = (LB, LB)
     right = (6, RB, RB)
     scratch = [
-        vm(left, f32), vm((4, RB, RB), f32), vm((256, 512), bf16), vm((512, 1024), f32), vm(left, f32),
+        vm((4, RB, RB), f32), vm((256, 512), bf16), vm((512, 1024), f32), vm(left, f32),
         vm((4, RB, RB), f32),
         vm((16, 512, 256), bf16), vm((16, 256, 1024), bf16), vm((512, 1024), f32),
-        *pair_of((512, 1024)), *pair_of((1024, 512)), *pair_of((1024, 512)), vm(left, f32),
+        *pair_of((1024, 512)), *pair_of((1024, 512)),
         vm(left, f32), vm(left, f32), *pair_of(left), *pair_of(left), *pair_of(left), *pair_of(left), *pair_of(left),
         *pair_of(left), *pair_of((512, 256)),
-        vm(right, f32), vm(right, f32), *pair_of(right), *pair_of(right), *pair_of(right), *pair_of(right),
-        *pair_of(right), *pair_of(right),
+        vm(right, f32), vm(right, f32), *pair_of((5, RB, RB)), *pair_of((5, RB, RB)), *pair_of((4, RB, RB)),
+        *pair_of((1, RB, RB)), *pair_of((4, RB, RB)), *pair_of((4, RB, RB)),
         vm((2, 4, 2, 64, 256), f32), vm((2, 6, 64, 256), f32), vm((2, 2, 64, 256), f32), vm((2, 4, 2, 16, 256), f32),
         vm((2, 6, 16, 256), f32), vm((2, 2, 16, 256), f32), vm((2, 4, 4, 2, 16, 256), f32),
         vm((2, 2, 4, 64, RB), f32), vm((2, 4, 64, RB), f32), vm((2, 4, 64, RB), f32), vm((6, 64, RB), f32),
         vm((2, 64, RB), f32), vm((2, 64, RB), f32), vm((2, 64, RB), f32), vm((4, 2, 64, RB), f32),
-        dma((16, 2)), dma((30,)), dma((16, 2)), dma((30,)), dma((6,)),
+        dma((16, 2)), dma((30,)), dma((16, 4)), dma((60,)), dma((6,)),
         dma((2, 6)), dma((2, 6)), dma((2, 4, 2)), dma((2, 4, 2)), dma((48,)),
-        dma((1,)), dma((6,)), dma((1,)), dma((4, 2)), dma((4,)), dma((24,)),
+        dma((1,)), dma((6,)), dma((1,)), dma((4, 2)), dma((4,)), dma((4, 2)), dma((24,)),
     ]
-    hbm = pl.BlockSpec(memory_space=pl.ANY)
+    hbm = pl.BlockSpec(memory_space=pltpu.HBM)
+    vmem = pl.BlockSpec(memory_space=pltpu.VMEM)
     return pl.pallas_call(
         comm_kernel,
         out_shape=(
@@ -611,50 +658,46 @@
             jax.ShapeDtypeStruct((4, RB, RB), f32),
         ),
         in_specs=[hbm] * 5,
-        out_specs=(hbm,) * 4,
+        out_specs=(vmem, vmem, vmem, hbm),
         scratch_shapes=scratch,
         compiler_params=pltpu.CompilerParams(
-            collective_id=1, has_side_effects=True, vmem_limit_bytes=60 * 1024 * 1024
+            collective_id=1, has_side_effects=True, vmem_limit_bytes=50 * 1024 * 1024
         ),
         name="comm",
     )(tok, grad, weight, left_param, right_param)
 
 
 def final_kernel(
-    wrh, wrl, nl, nr, out, nlo, nro, wh, wl, acc, nl_v, nr_v, S, A, sh, sl, ah, al, bh, bl, ch, cl, rh, rl, sem
+    wh, wl, nl_v, nr, out, nlo, nro, nr_v, acc, S, A, sh, sl, ah, al, bh, bl, ch, cl, rh, rl, sem
 ):
     def copy(src, dst, index):
         made = pltpu.make_async_copy(src, dst, sem.at[index])
         made.start()
         return made
 
-    left_in = copy(nl, nl_v, 0)
     right_in = copy(nr, nr_v, 1)
-    weight_in = [copy(wrh, wh, 2), copy(wrl, wl, 3)]
-    left_in.wait()
-    outs = [copy(nl_v, nlo, 4)]
+    outs = [copy(nl_v, nlo, 0)]
     param = nl_v[...]
     s = (0.5 / math.sqrt(LB)) * (param - param.T)
     S[...] = s
     put((sh, sl), s)
-    right_in.wait()
-    outs.append(copy(nr_v, nro, 5))
     poly(
         LB, 256, S, (sh, sl), (ah, al), (bh, bl), (ch, cl), A, lambda rows, value: put((rh, rl), value, rows)
     )
-    for made in weight_in:
-        made.wait()
+    right_in.wait()
+    outs.append(copy(nr_v, nro, 6))
     for index in range(4):
         cols = pl.ds(256 * index, 256)
         acc[:, cols] = dot3((rh[...], rl[...]), (wh[:, cols], wl[:, cols]))
-        outs.append(copy(acc.at[:, cols], out.at[:, cols], 6 + index))
+        outs.append(copy(acc.at[:, cols], out.at[:, cols], 2 + index))
     for made in outs:
         made.wait()
 
 
 def final_call(wrh, wrl, new_left, new_right):
     vm = pltpu.VMEM
-    hbm = pl.BlockSpec(memory_space=pl.ANY)
+    hbm = pl.BlockSpec(memory_space=pltpu.HBM)
+    vmem = pl.BlockSpec(memory_space=pltpu.VMEM)
     left = (LB, LB)
     return pl.pallas_call(
         final_kernel,
@@ -662,22 +705,26 @@
             jax.ShapeDtypeStruct(wrh.shape, f32), jax.ShapeDtypeStruct(left, f32),
             jax.ShapeDtypeStruct((4, RB, RB), f32),
         ),
-        in_specs=[hbm] * 4,
+        in_specs=[vmem, vmem, vmem, hbm],
         out_specs=(hbm,) * 3,
         scratch_shapes=[
-            *pair_of(wrh.shape), vm(wrh.shape, f32), vm(left, f32), vm((4, RB, RB), f32), vm(left, f32), vm(left, f32),
+            vm((4, RB, RB), f32), vm(wrh.shape, f32), vm(left, f32), vm(left, f32),
             *pair_of(left), *pair_of(left), *pair_of(left), *pair_of(left), *pair_of(left),
-            pltpu.SemaphoreType.DMA((10,)),
+            pltpu.SemaphoreType.DMA((7,)),
         ],
-        compiler_params=pltpu.CompilerParams(vmem_limit_bytes=60 * 1024 * 1024),
+        compiler_params=pltpu.CompilerParams(vmem_limit_bytes=24 * 1024 * 1024),
         name="final",
     )(wrh, wrl, new_left, new_right)
 
 
 def body(tokens, grad_out, base_weight, left_param, right_param):
     left = left_param.reshape(LB, LB)
+    tokens = pltpu.with_memory_space_constraint(tokens, pltpu.HBM)
+    grad_out = pltpu.with_memory_space_constraint(grad_out, pltpu.HBM)
     given = comm_call(tokens, grad_out, base_weight, left, right_param)
-    rotated, new_left, new_right = final_call(*given)
+    wrh, wrl, new_left, new_right = given
+    new_right = pltpu.with_memory_space_constraint(new_right, pltpu.HBM)
+    rotated, new_left, new_right = final_call(wrh, wrl, new_left, new_right)
     return rotated, new_left.reshape(1, LB, LB), new_right
 
 

time: 115 us -> 108 us (0.939)
  Pallas kernels: 114 us -> 107 us
    pallas_call x1, Pallas kernels: 105 us -> 99.7 us  [comm_call(): pl.pallas_call(comm_kernel, out_shape=(jax.ShapeDtypeStruct(weight.shape,...]
    pallas_call x1, Pallas kernels: 8.4 us -> 7.13 us  [final_call(): pl.pallas_call(final_kernel, out_shape=(jax.ShapeDtypeStruct(wrh.shape, f...]
where the time goes in v3:
time: 108 us
  Pallas kernels  107 us (99%)
    pallas_call x1, Pallas kernels, comm_call(): pl.pallas_call(comm_kernel, out_shape=(jax.ShapeDtypeStruct(weight.shape,...  99.7 us
    pallas_call x1, Pallas kernels, final_call(): pl.pallas_call(final_kernel, out_shape=(jax.ShapeDtypeStruct(wrh.shape, f...  7.13 us

profile of v3, /device:TPU:32, one launch (start us, length us, event | category | flops | bytes accessed | tf_op | source)
XLA Modules:
  0.0 107.7 jit_solution(1027879607022986757)
XLA Ops:
  0.6 99.7 %comm.1 = (bf16[512,1024]{1,0:T(8,128)(2,1)S(1)}, bf16[512,1024]{1,0:T(8,128)(2,1)S(1)}, f32[512,512]{1,0:T(8,128)S(1)}, f32[4,256,256]{2,1,0:T(8,128)}) custom-call(bf16[256,512]{1,0:T(8,128)(2,1)} %tok_hbm.1, bf16[256,1024]{1,0:T(8,128)(2,1)} %grad_ref.1, f32[512,1024]{1,0:T(8,128)} %w_hbm.1, f32[512,512]{1,0:T(8,128)} %bitcast.2, f32[4,256,256]{2,1,0:T(8,128)} %rp_hbm.1), custom_call_target="tpu_custom_call" | custom-call | tf_op jit(solution)/shard_map/comm/pallas_call | solution.py:653
  100.4 7.1 %final.1 = (f32[512,1024]{1,0:T(8,128)}, f32[512,512]{1,0:T(8,128)}, f32[4,256,256]{2,1,0:T(8,128)}) custom-call(bf16[512,1024]{1,0:T(8,128)(2,1)S(1)} %get-tuple-element.10.wh, bf16[512,1024]{1,0:T(8,128)(2,1)S(1)} %get-tuple-element.11.wl, f32[512,512]{1,0:T(8,128)S(1)} %get-tuple-element.12.nl_v, f32[4,256,256]{2,1,0:T(8,128)} %get-tuple-element.13.nr), custom_call_target="tpu_custom_call" | custom-call | tf_op jit(solution)/shard_map/final/pallas_call | solution.py:702

commit v4 on v3

--- a/solution.py
+++ b/solution.py
@@ -173,8 +173,6 @@
     barrier = pltpu.get_barrier_semaphore()
     for dev in (YP, YM, ZZ, CC, XP, XM, HP, HM):
         pl.semaphore_signal(barrier, inc=1, device_id=dev, device_id_type=pl.DeviceIdType.MESH)
-    load_tok.wait()
-    T[col] = tok_v[...].astype(f32).T.astype(bf16)
     pl.semaphore_wait(barrier, 8)
 
     def t_half(ref, half):
@@ -197,14 +195,16 @@
     def g_in(shard, half):
         arrive(g_half(Gr.at[shard], half), g_recv.at[shard, half])
 
+    for q in range(4):
+        g_go(row, q, YP, True)
+        g_go(row, (q + 2) % 4, YM, True)
+    load_tok.wait()
+    T[col] = tok_v[...].astype(f32).T.astype(bf16)
     for half in (0, 1):
         t_go(col, half, XP)
         t_go(col, 1 - half, XM)
         t_go(col, half, HP)
         t_go(col, 1 - half, HM)
-    for q in range(4):
-        g_go(row, q, YP, True)
-        g_go(row, (q + 2) % 4, YM, True)
     for q in (0, 2, 1):
         g_go(row, q, ZZ, True)
     for q in range(4):
@@ -333,7 +333,7 @@
             else:
                 gw[rows] = total
 
-        rows_loop(LB, 256, go)
+        rows_loop(LB, 512, go)
 
     def both(yy, zz):
         return [row_of(yy, zz, 0), row_of(yy, zz, 1)]
@@ -577,7 +577,7 @@
         def go(rows):
             gwh[rows, cols], gwl[rows, cols] = split(dot3(split(w_ref[rows, cols]), get(at(rRP, index))))
 
-        rows_loop(LB, 256, go)
+        rows_loop(LB, 512, go)
 
     def turn_other(zz):
         index = 2 * (1 - c) + zz
@@ -614,7 +614,7 @@
 
     join(pl.ds(0, 256))
     join(pl.ds(256, 256))
-    diff = adjoint_end(LB, 256, lCP, lSP, lAP, lRP, Ea, Aa, lA)
+    diff = adjoint_end(LB, 512, lCP, lSP, lAP, lRP, Ea, Aa, lA)
     nl_ref[...] = updated(lp_ref[...], diff, LB)
 
     for copy in started:
@@ -682,12 +682,12 @@
     S[...] = s
     put((sh, sl), s)
     poly(
-        LB, 256, S, (sh, sl), (ah, al), (bh, bl), (ch, cl), A, lambda rows, value: put((rh, rl), value, rows)
+        LB, 512, S, (sh, sl), (ah, al), (bh, bl), (ch, cl), A, lambda rows, value: put((rh, rl), value, rows)
     )
     right_in.wait()
     outs.append(copy(nr_v, nro, 6))
-    for index in range(4):
-        cols = pl.ds(256 * index, 256)
+    for index in range(2):
+        cols = pl.ds(512 * index, 512)
         acc[:, cols] = dot3((rh[...], rl[...]), (wh[:, cols], wl[:, cols]))
         outs.append(copy(acc.at[:, cols], out.at[:, cols], 2 + index))
     for made in outs:

time: 108 us -> 105 us (0.972)
  Pallas kernels: 107 us -> 104 us
    pallas_call x1, Pallas kernels: 99.7 us -> 97.8 us  [comm_call(): pl.pallas_call(comm_kernel, out_shape=(jax.ShapeDtypeStruct(weight.shape,...]
    pallas_call x1, Pallas kernels: 7.13 us -> 5.97 us  [final_call(): pl.pallas_call(final_kernel, out_shape=(jax.ShapeDtypeStruct(wrh.shape, f...]
where the time goes in v4:
time: 105 us
  Pallas kernels  104 us (99%)
    pallas_call x1, Pallas kernels, comm_call(): pl.pallas_call(comm_kernel, out_shape=(jax.ShapeDtypeStruct(weight.shape,...  97.8 us
    pallas_call x1, Pallas kernels, final_call(): pl.pallas_call(final_kernel, out_shape=(jax.ShapeDtypeStruct(wrh.shape, f...  5.97 us

profile of v4, /device:TPU:32, one launch (start us, length us, event | category | flops | bytes accessed | tf_op | source)
XLA Modules:
  0.0 104.6 jit_solution(9964248410185725760)
XLA Ops:
  0.6 97.8 %comm.1 = (bf16[512,1024]{1,0:T(8,128)(2,1)S(1)}, bf16[512,1024]{1,0:T(8,128)(2,1)S(1)}, f32[512,512]{1,0:T(8,128)S(1)}, f32[4,256,256]{2,1,0:T(8,128)}) custom-call(bf16[256,512]{1,0:T(8,128)(2,1)} %tok_hbm.1, bf16[256,1024]{1,0:T(8,128)(2,1)} %grad_ref.1, f32[512,1024]{1,0:T(8,128)} %w_hbm.1, f32[512,512]{1,0:T(8,128)} %bitcast.2, f32[4,256,256]{2,1,0:T(8,128)} %rp_hbm.1), custom_call_target="tpu_custom_call" | custom-call | tf_op jit(solution)/shard_map/comm/pallas_call | solution.py:653
  98.4 6.0 %final.1 = (f32[512,1024]{1,0:T(8,128)}, f32[512,512]{1,0:T(8,128)}, f32[4,256,256]{2,1,0:T(8,128)}) custom-call(bf16[512,1024]{1,0:T(8,128)(2,1)S(1)} %get-tuple-element.10.wh, bf16[512,1024]{1,0:T(8,128)(2,1)S(1)} %get-tuple-element.11.wl, f32[512,512]{1,0:T(8,128)S(1)} %get-tuple-element.12.nl_v, f32[4,256,256]{2,1,0:T(8,128)} %get-tuple-element.13.nr), custom_call_target="tpu_custom_call" | custom-call | tf_op jit(solution)/shard_map/final/pallas_call | solution.py:702

commit v5 on v4

--- a/solution.py
+++ b/solution.py
@@ -310,7 +310,7 @@
         g_far(2, z)
         g_pass(other, 0, YP, YM)
 
-    poly(LB, 256, lS, lSP, lAP, lBP, lCP, lA, lambda rows, value: put(lRP, value, rows), lCT, middle, early)
+    poly(LB, 512, lS, lSP, lAP, lBP, lCP, lA, lambda rows, value: put(lRP, value, rows), lCT, middle, early)
     g_far(1, z)
     g_far(3, z)
     g_pass(other, 2, YM, YP)
@@ -686,8 +686,8 @@
     )
     right_in.wait()
     outs.append(copy(nr_v, nro, 6))
-    for index in range(2):
-        cols = pl.ds(512 * index, 512)
+    for index, (start, width) in enumerate(((0, 512), (512, 256), (768, 256))):
+        cols = pl.ds(start, width)
         acc[:, cols] = dot3((rh[...], rl[...]), (wh[:, cols], wl[:, cols]))
         outs.append(copy(acc.at[:, cols], out.at[:, cols], 2 + index))
     for made in outs:

time: 105 us -> 104 us (level)
  no operation moved by 1% of the time
where the time goes in v5:
time: 104 us
  Pallas kernels  104 us (100%)
    pallas_call x1, Pallas kernels, comm_call(): pl.pallas_call(comm_kernel, out_shape=(jax.ShapeDtypeStruct(weight.shape,...  97.6 us
    pallas_call x1, Pallas kernels, final_call(): pl.pallas_call(final_kernel, out_shape=(jax.ShapeDtypeStruct(wrh.shape, f...  5.97 us

profile of v5, /device:TPU:32, one launch (start us, length us, event | category | flops | bytes accessed | tf_op | source)
XLA Modules:
  0.0 104.4 jit_solution(5817782600897036993)
XLA Ops:
  0.6 97.6 %comm.1 = (bf16[512,1024]{1,0:T(8,128)(2,1)S(1)}, bf16[512,1024]{1,0:T(8,128)(2,1)S(1)}, f32[512,512]{1,0:T(8,128)S(1)}, f32[4,256,256]{2,1,0:T(8,128)}) custom-call(bf16[256,512]{1,0:T(8,128)(2,1)} %tok_hbm.1, bf16[256,1024]{1,0:T(8,128)(2,1)} %grad_ref.1, f32[512,1024]{1,0:T(8,128)} %w_hbm.1, f32[512,512]{1,0:T(8,128)} %bitcast.2, f32[4,256,256]{2,1,0:T(8,128)} %rp_hbm.1), custom_call_target="tpu_custom_call" | custom-call | tf_op jit(solution)/shard_map/comm/pallas_call | solution.py:653
  98.3 6.0 %final.1 = (f32[512,1024]{1,0:T(8,128)}, f32[512,512]{1,0:T(8,128)}, f32[4,256,256]{2,1,0:T(8,128)}) custom-call(bf16[512,1024]{1,0:T(8,128)(2,1)S(1)} %get-tuple-element.10.wh, bf16[512,1024]{1,0:T(8,128)(2,1)S(1)} %get-tuple-element.11.wl, f32[512,512]{1,0:T(8,128)S(1)} %get-tuple-element.12.nl_v, f32[4,256,256]{2,1,0:T(8,128)} %get-tuple-element.13.nr), custom_call_target="tpu_custom_call" | custom-call | tf_op jit(solution)/shard_map/final/pallas_call | solution.py:702
